TPU v7x, 512 devices: a whole 4x4x16 slice. The times are simulated.
512 devices in a mesh: seq: 64 (over z_lo, y, core), head: 8 (over x, z_hi).
Axes of the slice: x: 4, y: 4, z: 16 (z_hi: 2, z_lo: 8; z = z_hi * 8 + z_lo), core: 2. Of those that a mesh axis runs over, the one named last changes fastest.
Arguments:
- block_input: bfloat16 [18432, 3072], P('seq', 'head'), may hold values from -6 to 6
- mod_shift: float32 [3072], replicated, may hold values from -1.2 to 1.2
- mod_scale: float32 [3072], replicated, may hold values from -0.8 to 0.8
- history: float32 [16], replicated, may hold values from 3 to 6
- w_qkv: bfloat16 [3, 3072, 3072], P(None, 'seq', 'head')
- pattern: int32 [192, 12], P('seq'), may hold values from 0 to 191, as said below
- out_cotangent: bfloat16 [18432, 3072], P('seq', 'head'), may hold values from -6 to 6
Outputs:
- attn_out: bfloat16 [18432, 3072], P('seq', 'head')
- grad_qkv: bfloat16 [3, 18432, 3072], P(None, 'seq', 'head')
- new_history: float32 [16], replicated
Inputs may be any that keep to these rules, and one draw needn't show every extreme that they name: `pattern`: row a lists 12 distinct tiles, the first being tile a itself; every listed tile lies in a's frame or the frame just before or after it, in a's tile row or the row just above or below it within the frame, and in a window of 3 tile columns around a's column, the window moved inward at a frame's side edges.
All inputs are finite; a program needn't handle non-finite values.
Results may differ from a plain program's by a relative error of at most 0.0096.
Values may be sent and summed in bfloat16 or wider, within the bound.
A program may use at most 64 MiB of HBM per device.

v0:
```python
import jax
import jax.numpy as jnp
from jax import lax
from jax.sharding import PartitionSpec as P

HD = 128
TILE = 96
GRID_H = 8


LIMIT = 448.0
EPSILON = 1e-06


def from_behind(x, axis, by):
    peers = lax.axis_size(axis)
    pairs = [(i, i + by) for i in range(peers) if 0 <= i + by < peers]
    return lax.ppermute(x, axis, pairs)


def modulate(full_rows, shift_vec, scale_vec):
    row_mean = jnp.mean(full_rows, axis=1, keepdims=True)
    row_square = jnp.mean(full_rows * full_rows, axis=1, keepdims=True)
    normed = (full_rows - row_mean) * lax.rsqrt(row_square - row_mean * row_mean + EPSILON)
    return normed * (1.0 + scale_vec) + shift_vec


def attend_head(query_tile, key_tile, value_tile, grad_out, onehot, inv_root):
    scores = (
        jnp.einsum("aqd,akd->aqk", query_tile, key_tile, preferred_element_type=jnp.float32)
        * inv_root
    )
    row_max = jnp.max(scores, axis=2, keepdims=True)
    weights = jnp.exp(scores - row_max)
    softmax_w = weights / jnp.sum(weights, axis=2, keepdims=True)
    softmax_low = softmax_w.astype(jnp.bfloat16)
    output = jnp.einsum("aqk,akd->aqd", softmax_low, value_tile, preferred_element_type=jnp.float32)
    grad_prob = jnp.einsum("aqd,akd->aqk", grad_out, value_tile, preferred_element_type=jnp.float32)
    row_delta = jnp.sum(softmax_w * grad_prob, axis=2, keepdims=True)
    grad_score = (softmax_w * (grad_prob - row_delta)).astype(jnp.bfloat16)
    grad_query = (
        jnp.einsum("aqk,akd->aqd", grad_score, key_tile, preferred_element_type=jnp.float32)
        * inv_root
    )
    tiles_here = query_tile.shape[0]
    tile_len = query_tile.shape[1]
    slot_count = onehot.shape[1]
    score_slots = grad_score.reshape(tiles_here, tile_len, slot_count, tile_len)
    prob_slots = softmax_low.reshape(tiles_here, tile_len, slot_count, tile_len)
    score_window = jnp.einsum(
        "aqsk,asw->aqwk", score_slots, onehot, preferred_element_type=jnp.float32
    ).astype(jnp.bfloat16)
    prob_window = jnp.einsum(
        "aqsk,asw->aqwk", prob_slots, onehot, preferred_element_type=jnp.float32
    ).astype(jnp.bfloat16)
    key_window = (
        jnp.einsum("aqwk,aqd->wkd", score_window, query_tile, preferred_element_type=jnp.float32)
        * inv_root
    )
    value_window = jnp.einsum(
        "aqwk,aqd->wkd", prob_window, grad_out, preferred_element_type=jnp.float32
    )
    return (output, grad_query, jnp.stack([key_window, value_window], axis=0))


def local(block_input, mod_shift, mod_scale, history, w_qkv, pattern, out_cotangent):
    peak_value = jnp.max(history)
    scale_up = LIMIT / peak_value
    scale_down = peak_value / LIMIT
    rows_here = block_input.shape[0]
    full_rows = lax.all_gather(block_input, "head", axis=1, tiled=True)
    modulated = modulate(full_rows.astype(jnp.float32), mod_shift, mod_scale)
    abs_peak = lax.pmax(jnp.max(jnp.abs(modulated)), "seq")
    full_quant = jnp.clip(modulated * scale_up, -LIMIT, LIMIT).astype(jnp.bfloat16)
    new_history = jnp.concatenate([abs_peak.reshape(1), history[:-1]])
    feature_count = w_qkv.shape[2]
    full_weight = lax.all_gather(w_qkv, "seq", axis=1, tiled=True)
    projected = jnp.stack(
        [
            jnp.dot(full_quant, full_weight[which], preferred_element_type=jnp.float32)
            for which in range(3)
        ],
        axis=0,
    )
    qkv = (projected * scale_down).astype(jnp.bfloat16)
    heads_here = feature_count // HD
    tiles_here = rows_here // TILE
    key_pairs = qkv[1:]
    slab_list = []
    for frame_step in (-1, 0, 1):
        for row_step in (-1, 0, 1):
            offset_slab = frame_step * GRID_H + row_step
            if offset_slab == 0:
                slab_list.append(key_pairs)
            else:
                slab_list.append(from_behind(key_pairs, "seq", -offset_slab))
    extended = jnp.stack(slab_list, axis=0)
    ext_tiles = extended.reshape(9, 2, tiles_here, TILE, heads_here, HD)
    own_index = lax.axis_index("seq")
    tile_offset = pattern // tiles_here - own_index
    frame_of = (tile_offset + 1) // GRID_H
    slot_of = (frame_of + 1) * 3 + tile_offset - frame_of * GRID_H + 1
    local_ids = (slot_of * tiles_here + pattern % tiles_here).reshape(-1)
    window_count = 9 * tiles_here
    onehot = (local_ids[:, None] == jnp.arange(window_count, dtype=jnp.int32)[None, :]).astype(
        jnp.bfloat16
    )
    onehot = onehot.reshape(tiles_here, -1, window_count)
    query_all = qkv[0].reshape(tiles_here, TILE, heads_here, HD)
    grad_all = out_cotangent.reshape(tiles_here, TILE, heads_here, HD)
    inv_root = HD ** (-0.5)
    outputs = []
    grad_queries = []
    grad_backs = []
    for which_head in range(heads_here):
        head_ext = (
            ext_tiles[:, :, :, :, which_head]
            .transpose(1, 0, 2, 3, 4)
            .reshape(2, window_count, TILE, HD)
        )
        head_pairs = jnp.take(head_ext, local_ids, axis=1).reshape(2, tiles_here, -1, HD)
        output, grad_query, returned = attend_head(
            query_all[:, :, which_head],
            head_pairs[0],
            head_pairs[1],
            grad_all[:, :, which_head],
            onehot,
            inv_root,
        )
        outputs.append(output)
        grad_queries.append(grad_query)
        grad_backs.append(returned)
    attn_out = jnp.stack(outputs, axis=2).reshape(rows_here, feature_count).astype(jnp.bfloat16)
    grad_query = jnp.stack(grad_queries, axis=2).reshape(rows_here, feature_count)
    grad_ext = jnp.stack(grad_backs, axis=3).reshape(2, 9, rows_here, feature_count)
    partials = lax.optimization_barrier(grad_ext.astype(jnp.bfloat16))
    grad_total = partials[:, 4].astype(jnp.float32)
    for frame_step in (-1, 0, 1):
        for row_step in (-1, 0, 1):
            offset_slab = frame_step * GRID_H + row_step
            if offset_slab != 0:
                slot_index = (frame_step + 1) * 3 + row_step + 1
                piece = partials[:, slot_index]
                arrived = from_behind(piece, "seq", offset_slab)
                grad_total = grad_total + arrived.astype(jnp.float32)
    grad_qkv = jnp.concatenate([grad_query[None], grad_total], axis=0).astype(jnp.bfloat16)
    return (attn_out, grad_qkv, new_history)


def solution(mesh):
    placed = (
        P("seq", "head"),
        P(),
        P(),
        P(),
        P(None, "seq", "head"),
        P("seq", None),
        P("seq", "head"),
    )
    return jax.shard_map(
        local,
        mesh=mesh,
        in_specs=placed,
        out_specs=(P("seq", "head"), P(None, "seq", "head"), P()),
        check_vma=False,
    )
```

profile of v0, /device:TPU:1, one launch (start us, length us, event | category | flops | bytes accessed | tf_op | source)
XLA Modules:
  0.0 719.9 jit_solution(15918916557093568611)
XLA Ops:
  14.9 108.9 %all-gather.3.cloned.1.call-done = bf16[288,3072]{1,0:T(8,128)(2,1)} async-done(((bf16[288,384]{1,0:T(8,128)(2,1)}), bf16[288,3072]{1,0:T(8,128)(2,1)}) %all-gather.3.cloned.1.call-update) | async-done | bytes 1769488 | tf_op jit(solution)/shard_map/all_gather | solution.py:71
  123.8 2.2 convert_reduce_fusion
  126.0 120.7 %all-gather.5.cloned.1.call-done = bf16[3,3072,384]{2,1,0:T(8,128)(2,1)} async-done(((bf16[3,48,384]{2,1,0:T(8,128)(2,1)}), bf16[3,3072,384]{2,1,0:T(8,128)(2,1)}) %all-gather.5.cloned.1.call-update) | async-done | bytes 7077904 | tf_op jit(solution)/shard_map/all_gather | solution.py:77
  246.7 2.9 fusion.103
  253.0 3.3 collective-permute-start
  256.2 2.5 collective-permute-start.1
  260.1 213.6 %pmax.7 = f32[1]{0:T(128)} all-reduce(f32[1]{0:T(128)} %bitcast.87), channel_id=1, replica_groups=mesh['seq'=64,'head'=8] {'seq'}, use_global_device_ids=true, to_apply=%region_13.15 | all-reduce | flops 1 | bytes 8 | tf_op jit(solution)/shard_map/pmax | solution.py:73
  475.0 2.1 collective-permute-start.2
  477.0 3.3 collective-permute-start.3
  480.4 11.5 %collective-permute-start.4 = (bf16[2,288,384]{2,1,0:T(8,128)(2,1)S(1)}, bf16[2,288,384]{2,1,0:T(8,128)(2,1)S(1)}, u32[]{:S(2)}, u32[]{:S(2)}) collective-permute-start(bf16[2,288,384]{2,1,0:T(8,128)(2,1)S(1)} %slice.137), channel_id=1, source_target_pairs={{8,0},{16,8},{24,16},{32,24},{40,32},{48,40},{56,48},{64,56},{72,6... | collective-permute-start | bytes 1327112 | tf_op jit(solution)/shard_map/ppermute | solution.py:18
  494.4 1.4 stack.130
  497.2 1.4 stack.131
  500.7 1.5 collective-permute-start.7
  502.1 1.4 stack.132
  503.6 1.4 stack.133
  508.4 2.7 collective-permute-done.6
  518.1 10.9 %fusion.201 = (bf16[9,2,3,96,1,128]{5,4,3,2,1,0:T(2,128)(2,1)S(1)}, bf16[9,2,3,96,1,128]{5,4,3,2,1,0:T(2,128)(2,1)S(1)}, bf16[9,2,3,96,1,128]{5,4,3,2,1,0:T(2,128)(2,1)S(1)}) fusion(bf16[9,2,3,96,3,128]{5,4,3,2,1,0:T(4,128)(2,1)} %constant_dynamic-update-slice_fusion), kind=kLoop, calls=%fused_computation.212 | loop fusion | bytes 7962624 | tf_op jit(solution)/shard_map/slice | solution.py:117
  531.4 3.5 gather_fusion
  534.9 3.4 gather_fusion.1
  539.6 3.6 gather_fusion.2
  543.2 2.5 select_bitcast_fusion.2
  545.7 2.0 fusion.202
  547.7 2.6 fusion.213
  550.4 2.3 multiply_reduce_fusion.2
  555.7 2.4 copy.24
  558.1 2.6 fusion.210
  560.7 2.0 multiply_reduce_fusion.1
  567.6 2.0 copy.40
  569.5 2.2 fusion.158
  571.7 3.3 copy.41
  575.0 3.2 fusion.91
  578.7 1.8 copy.43
  580.4 2.1 fusion.156
  582.6 3.3 copy.44
  585.9 3.2 fusion.94
  589.1 1.7 copy.46
  590.9 2.2 fusion.154
  593.0 3.3 copy.47
  596.3 3.2 fusion.88
  600.0 1.8 copy.49
  601.8 2.2 fusion.152
  603.9 3.7 copy.50
  607.6 3.2 fusion.97
  611.7 1.7 multiply_reduce_fusion
  615.4 1.7 copy.52
  617.2 2.2 fusion.150
  619.3 3.3 copy.53
  622.6 3.2 fusion.85
  626.3 1.8 copy.55
  628.1 2.2 fusion.148
  630.2 3.3 copy.56
  633.5 2.4 fusion.100
  639.0 5.8 copy.30
  644.7 11.1 %convert_element_type.125 = bf16[2,9,288,384]{3,2,1,0:T(8,128)(2,1)} reshape(bf16[2,27,96,3,128]{4,3,2,1,0:T(4,128)(2,1)} %copy.30) | data formatting | bytes 7962624 | tf_op jit(solution)/shard_map/convert_element_type | solution.py:136
  655.8 3.8 slice_bitcast_fusion.19
  661.1 8.9 %collective-permute-start.11 = (bf16[2,288,384]{2,1,0:T(8,128)(2,1)}, bf16[2,288,384]{2,1,0:T(8,128)(2,1)}, u32[]{:S(2)}, u32[]{:S(2)}) collective-permute-start(bf16[2,288,384]{2,1,0:T(8,128)(2,1)} %get-tuple-element.12), channel_id=1, source_target_pairs={{8,0},{16,8},{24,16},{32,24},{40,32},{48,40},{56,48},{64,56},{72,6... | collective-permute-start | bytes 1327112 | tf_op jit(solution)/shard_map/ppermute | solution.py:18
  670.1 1.9 collective-permute-start.12
  672.8 6.7 collective-permute-start.13
  680.9 1.5 fusion.109
  686.3 1.5 fusion.110
  689.2 5.6 collective-permute-done.14
  694.7 9.3 %collective-permute-done.15 = bf16[2,288,384]{2,1,0:T(8,128)(2,1)S(1)} collective-permute-done((bf16[2,288,384]{2,1,0:T(8,128)(2,1)}, bf16[2,288,384]{2,1,0:T(8,128)(2,1)S(1)}, u32[]{:S(2)}, u32[]{:S(2)}) %collective-permute-start.15) | collective-permute-done | bytes 442400 | tf_op jit(solution)/shard_map/ppermute | solution.py:18
  704.0 6.0 collective-permute-done.9
  710.0 1.9 fusion.122
  (150 shorter events, 56.8 us)
Async XLA Ops:
  7.2 239.5 %copy-start.30 = (f32[3072]{0:T(1024)S(1)}, f32[3072]{0:T(1024)}, u32[]{:S(2)}) copy-start(f32[3072]{0:T(1024)} %param.10) | copy-start | bytes 36868
  7.2 116.6 %all-gather.3.cloned.1.call-start = ((), (), s32[]{:S(2)}) async-start(), calls=%async_computation | async-start | bytes 1990656 | tf_op jit(solution)/shard_map/all_gather | solution.py:71
  7.9 238.8 %all-gather.5.cloned.1.call-start = ((), (), s32[]{:S(2)}) async-start(), calls=%async_computation.1 | async-start | bytes 7188480 | tf_op jit(solution)/shard_map/all_gather | solution.py:77
  123.8 122.9 %copy-start = (bf16[288,3072]{1,0:T(8,128)(2,1)S(1)}, bf16[288,3072]{1,0:T(8,128)(2,1)}, u32[]{:S(2)}) copy-start(bf16[288,3072]{1,0:T(8,128)(2,1)} %all-gather.3.cloned.1.call-done) | copy-start | bytes 5308420
  246.7 3.7 copy-start.31
  252.9 220.8 %copy-start.32 = (f32[16]{0:T(128)S(1)}, f32[16]{0:T(128)}, u32[]{:S(2)}) copy-start(f32[16]{0:T(128)} %param.12) | copy-start | bytes 196
  253.0 240.2 %collective-permute-start = (bf16[2,288,384]{2,1,0:T(8,128)(2,1)S(1)}, bf16[2,288,384]{2,1,0:T(8,128)(2,1)}, u32[]{:S(2)}, u32[]{:S(2)}) collective-permute-start(bf16[2,288,384]{2,1,0:T(8,128)(2,1)S(1)} %slice.137), channel_id=1, source_target_pairs={{0,72},{8,80},{16,88},{24,96},{32,104},{40,112},{48,120},{56,128},... | collective-permute-start | bytes 1327112 | tf_op jit(solution)/shard_map/ppermute | solution.py:18
  256.2 239.6 %collective-permute-start.1 = (bf16[2,288,384]{2,1,0:T(8,128)(2,1)S(1)}, bf16[2,288,384]{2,1,0:T(8,128)(2,1)}, u32[]{:S(2)}, u32[]{:S(2)}) collective-permute-start(bf16[2,288,384]{2,1,0:T(8,128)(2,1)S(1)} %slice.137), channel_id=1, source_target_pairs={{0,64},{8,72},{16,80},{24,88},{32,96},{40,104},{48,112},{56,120},{... | collective-permute-start | bytes 1327112 | tf_op jit(solution)/shard_map/ppermute | solution.py:18
  475.0 25.7 %collective-permute-start.2 = (bf16[2,288,384]{2,1,0:T(8,128)(2,1)S(1)}, bf16[2,288,384]{2,1,0:T(8,128)(2,1)}, u32[]{:S(2)}, u32[]{:S(2)}) collective-permute-start(bf16[2,288,384]{2,1,0:T(8,128)(2,1)S(1)} %slice.137), channel_id=1, source_target_pairs={{0,56},{8,64},{16,72},{24,80},{32,88},{40,96},{48,104},{56,112},{6... | collective-permute-start | bytes 1327112 | tf_op jit(solution)/shard_map/ppermute | solution.py:18
  477.0 26.6 %collective-permute-start.3 = (bf16[2,288,384]{2,1,0:T(8,128)(2,1)S(1)}, bf16[2,288,384]{2,1,0:T(8,128)(2,1)}, u32[]{:S(2)}, u32[]{:S(2)}) collective-permute-start(bf16[2,288,384]{2,1,0:T(8,128)(2,1)S(1)} %slice.137), channel_id=1, source_target_pairs={{0,8},{8,16},{16,24},{24,32},{32,40},{40,48},{48,56},{56,64},{64,7... | collective-permute-start | bytes 1327112 | tf_op jit(solution)/shard_map/ppermute | solution.py:18
  480.4 27.7 %collective-permute-start.4 = (bf16[2,288,384]{2,1,0:T(8,128)(2,1)S(1)}, bf16[2,288,384]{2,1,0:T(8,128)(2,1)S(1)}, u32[]{:S(2)}, u32[]{:S(2)}) collective-permute-start(bf16[2,288,384]{2,1,0:T(8,128)(2,1)S(1)} %slice.137), channel_id=1, source_target_pairs={{8,0},{16,8},{24,16},{32,24},{40,32},{48,40},{56,48},{64,56},{72,6... | collective-permute-start | bytes 1327112 | tf_op jit(solution)/shard_map/ppermute | solution.py:18
  493.1 15.1 %collective-permute-start.5 = (bf16[2,288,384]{2,1,0:T(8,128)(2,1)S(1)}, bf16[2,288,384]{2,1,0:T(8,128)(2,1)S(1)}, u32[]{:S(2)}, u32[]{:S(2)}) collective-permute-start(bf16[2,288,384]{2,1,0:T(8,128)(2,1)S(1)} %slice.137), channel_id=1, source_target_pairs={{56,0},{64,8},{72,16},{80,24},{88,32},{96,40},{104,48},{112,56},{1... | collective-permute-start | bytes 1327112 | tf_op jit(solution)/shard_map/ppermute | solution.py:18
  495.9 15.2 %collective-permute-start.6 = (bf16[2,288,384]{2,1,0:T(8,128)(2,1)S(1)}, bf16[2,288,384]{2,1,0:T(8,128)(2,1)}, u32[]{:S(2)}, u32[]{:S(2)}) collective-permute-start(bf16[2,288,384]{2,1,0:T(8,128)(2,1)S(1)} %slice.137), channel_id=1, source_target_pairs={{64,0},{72,8},{80,16},{88,24},{96,32},{104,40},{112,48},{120,56},{... | collective-permute-start | bytes 1327112 | tf_op jit(solution)/shard_map/ppermute | solution.py:18
  500.7 14.9 %collective-permute-start.7 = (bf16[2,288,384]{2,1,0:T(8,128)(2,1)S(1)}, bf16[2,288,384]{2,1,0:T(8,128)(2,1)}, u32[]{:S(2)}, u32[]{:S(2)}) collective-permute-start(bf16[2,288,384]{2,1,0:T(8,128)(2,1)S(1)} %slice.137), channel_id=1, source_target_pairs={{72,0},{80,8},{88,16},{96,24},{104,32},{112,40},{120,48},{128,56},... | collective-permute-start | bytes 1327112 | tf_op jit(solution)/shard_map/ppermute | solution.py:18
  539.6 3.6 copy-start.1
  550.4 2.3 copy-start.12
  553.8 0.8 copy-start.10
  555.7 5.1 copy-start.14
  560.7 2.0 copy-start.11
  566.1 1.5 copy-start.15
  571.7 3.3 copy-start.24
  575.0 3.2 copy-start.4
  582.6 3.3 copy-start.27
  585.9 3.2 copy-start.16
  593.0 3.3 copy-start.23
  596.3 3.2 copy-start.2
  603.9 3.7 copy-start.26
  607.6 3.2 copy-start.22
  610.8 0.9 copy-start.25
  614.6 0.9 copy-start.8
  622.6 3.2 copy-start.6
  633.5 2.4 copy-start.17
  633.5 2.4 copy-start.18
  636.0 1.1 copy-start.19
  636.0 1.3 copy-start.20
  637.3 1.1 copy-start.21
  655.8 16.1 %copy-start.9 = (bf16[3,96,1152]{2,1,0:T(8,128)(2,1)S(1)}, bf16[3,96,1152]{2,1,0:T(8,128)(2,1)}, u32[]{:S(2)}) copy-start(bf16[3,96,1152]{2,1,0:T(8,128)(2,1)} %copy-done.8) | copy-start | bytes 1990660
  655.8 16.5 %copy-start.28 = (bf16[3,96,1,128]{3,1,0,2:T(8,128)(2,1)S(1)}, bf16[3,96,1,128]{3,1,0,2:T(8,128)(2,1)}, u32[]{:S(2)}) copy-start(bf16[3,96,1,128]{3,1,0,2:T(8,128)(2,1)} %fusion.114) | copy-start | bytes 221188
  655.8 16.5 %copy-start.29 = (bf16[3,96,1,128]{3,1,0,2:T(8,128)(2,1)S(1)}, bf16[3,96,1,128]{3,1,0,2:T(8,128)(2,1)}, u32[]{:S(2)}) copy-start(bf16[3,96,1,128]{3,1,0,2:T(8,128)(2,1)} %fusion.113) | copy-start | bytes 221188
  659.7 21.2 %copy-start.5 = (bf16[3,96,1152]{2,1,0:T(8,128)(2,1)S(1)}, bf16[3,96,1152]{2,1,0:T(8,128)(2,1)}, u32[]{:S(2)}) copy-start(bf16[3,96,1152]{2,1,0:T(8,128)(2,1)} %get-tuple-element.24) | copy-start | bytes 1990660
  659.7 22.7 %collective-permute-start.10 = (bf16[2,288,384]{2,1,0:T(8,128)(2,1)}, bf16[2,288,384]{2,1,0:T(8,128)(2,1)}, u32[]{:S(2)}, u32[]{:S(2)}) collective-permute-start(bf16[2,288,384]{2,1,0:T(8,128)(2,1)} %get-tuple-element.13), channel_id=1, source_target_pairs={{56,0},{64,8},{72,16},{80,24},{88,32},{96,40},{104,48},{112,56},{1... | collective-permute-start | bytes 1327112 | tf_op jit(solution)/shard_map/ppermute | solution.py:18
  661.1 22.6 %collective-permute-start.11 = (bf16[2,288,384]{2,1,0:T(8,128)(2,1)}, bf16[2,288,384]{2,1,0:T(8,128)(2,1)}, u32[]{:S(2)}, u32[]{:S(2)}) collective-permute-start(bf16[2,288,384]{2,1,0:T(8,128)(2,1)} %get-tuple-element.12), channel_id=1, source_target_pairs={{8,0},{16,8},{24,16},{32,24},{40,32},{48,40},{56,48},{64,56},{72,6... | collective-permute-start | bytes 1327112 | tf_op jit(solution)/shard_map/ppermute | solution.py:18
  670.1 15.0 %collective-permute-start.12 = (bf16[2,288,384]{2,1,0:T(8,128)(2,1)}, bf16[2,288,384]{2,1,0:T(8,128)(2,1)}, u32[]{:S(2)}, u32[]{:S(2)}) collective-permute-start(bf16[2,288,384]{2,1,0:T(8,128)(2,1)} %get-tuple-element.11), channel_id=1, source_target_pairs={{0,8},{8,16},{16,24},{24,32},{32,40},{40,48},{48,56},{56,64},{64,7... | collective-permute-start | bytes 1327112 | tf_op jit(solution)/shard_map/ppermute | solution.py:18
  672.4 14.0 %copy-start.3 = (bf16[3,96,1152]{2,1,0:T(8,128)(2,1)S(1)}, bf16[3,96,1152]{2,1,0:T(8,128)(2,1)}, u32[]{:S(2)}) copy-start(bf16[3,96,1152]{2,1,0:T(8,128)(2,1)} %get-tuple-element.26) | copy-start | bytes 1990660
  672.6 15.3 %copy-start.7 = (bf16[3,96,1152]{2,1,0:T(8,128)(2,1)S(1)}, bf16[3,96,1152]{2,1,0:T(8,128)(2,1)}, u32[]{:S(2)}) copy-start(bf16[3,96,1152]{2,1,0:T(8,128)(2,1)} %get-tuple-element.28) | copy-start | bytes 1990660
  672.6 15.3 %copy-start.13 = (bf16[1,36,96,128]{3,2,0,1:T(8,128)(2,1)S(1)}, bf16[1,36,96,128]{3,2,0,1:T(8,128)(2,1)}, u32[]{:S(2)}) copy-start(bf16[1,36,96,128]{3,2,0,1:T(8,128)(2,1)} %get-tuple-element.21) | copy-start | bytes 2654212
  672.8 16.4 %collective-permute-start.13 = (bf16[2,288,384]{2,1,0:T(8,128)(2,1)}, bf16[2,288,384]{2,1,0:T(8,128)(2,1)S(1)}, u32[]{:S(2)}, u32[]{:S(2)}) collective-permute-start(bf16[2,288,384]{2,1,0:T(8,128)(2,1)} %get-tuple-element.10), channel_id=1, source_target_pairs={{0,56},{8,64},{16,72},{24,80},{32,88},{40,96},{48,104},{56,112},{6... | collective-permute-start | bytes 1327112 | tf_op jit(solution)/shard_map/ppermute | solution.py:18
  679.5 15.2 %collective-permute-start.14 = (bf16[2,288,384]{2,1,0:T(8,128)(2,1)}, bf16[2,288,384]{2,1,0:T(8,128)(2,1)S(1)}, u32[]{:S(2)}, u32[]{:S(2)}) collective-permute-start(bf16[2,288,384]{2,1,0:T(8,128)(2,1)} %get-tuple-element.16), channel_id=1, source_target_pairs={{0,64},{8,72},{16,80},{24,88},{32,96},{40,104},{48,112},{56,120},{... | collective-permute-start | bytes 1327112 | tf_op jit(solution)/shard_map/ppermute | solution.py:18
  682.4 21.6 %collective-permute-start.15 = (bf16[2,288,384]{2,1,0:T(8,128)(2,1)}, bf16[2,288,384]{2,1,0:T(8,128)(2,1)S(1)}, u32[]{:S(2)}, u32[]{:S(2)}) collective-permute-start(bf16[2,288,384]{2,1,0:T(8,128)(2,1)} %get-tuple-element.15), channel_id=1, source_target_pairs={{0,72},{8,80},{16,88},{24,96},{32,104},{40,112},{48,120},{56,128},... | collective-permute-start | bytes 1327112 | tf_op jit(solution)/shard_map/ppermute | solution.py:18
  683.7 20.3 %collective-permute-start.8 = (bf16[2,288,384]{2,1,0:T(8,128)(2,1)}, bf16[2,288,384]{2,1,0:T(8,128)(2,1)S(1)}, u32[]{:S(2)}, u32[]{:S(2)}) collective-permute-start(bf16[2,288,384]{2,1,0:T(8,128)(2,1)} %get-tuple-element.9), channel_id=1, source_target_pairs={{72,0},{80,8},{88,16},{96,24},{104,32},{112,40},{120,48},{128,56},... | collective-permute-start | bytes 1327112 | tf_op jit(solution)/shard_map/ppermute | solution.py:18
  685.0 25.0 %collective-permute-start.9 = (bf16[2,288,384]{2,1,0:T(8,128)(2,1)}, bf16[2,288,384]{2,1,0:T(8,128)(2,1)S(1)}, u32[]{:S(2)}, u32[]{:S(2)}) collective-permute-start(bf16[2,288,384]{2,1,0:T(8,128)(2,1)} %get-tuple-element.14), channel_id=1, source_target_pairs={{64,0},{72,8},{80,16},{88,24},{96,32},{104,40},{112,48},{120,56},{... | collective-permute-start | bytes 1327112 | tf_op jit(solution)/shard_map/ppermute | solution.py:18
Sparse Core Ops, SparseCore 0:
  11.1 112.6 all-gather.2
  125.9 120.7 all-gather.4
where the time goes:
time: 734 us; the launch traced here: 720 us
  waiting for transfers between devices  255 us (35%)
  blocking collectives  214 us (29%)
  local copies, waits for them, and re-layouts  113 us (15%)
  matrix products  54.4 us (7%)
  starting transfers between devices  50.9 us (7%)
  other arithmetic  17.4 us (2%)
  between operations  16.3 us (2%)
    pmax x1, blocking collectives, local(): abs_peak = lax.pmax(jnp.max(jnp.abs(modulated)), 'seq')  214 us
    all_gather x1, waiting for transfers between devices, local(): full_weight = lax.all_gather(w_qkv, 'seq', axis=1, tiled=True)  121 us
    all_gather x1, waiting for transfers between devices, local(): full_rows = lax.all_gather(block_input, 'head', axis=1, tiled=True)  109 us
    ppermute x16, starting transfers between devices, from_behind(): return lax.ppermute(x, axis, pairs)  50.8 us
    ppermute x16, waiting for transfers between devices, from_behind(): return lax.ppermute(x, axis, pairs)  23.6 us
  transfers between devices with their start and end apart: 18, of which 6 were waited for; matrix products, arithmetic and copies ran while one was open for 4% of the time, Pallas kernels for 0%

commit v1 on v0

v1 whole, which is shorter than its diff:
```python
import functools
import math

import jax
import jax.numpy as jnp
from jax import lax
from jax.experimental import pallas as pl
from jax.experimental.pallas import tpu as pltpu
from jax.sharding import PartitionSpec as P

HD = 128
TILE = 96
GRID_H = 8
NY = 4
NZ = 8
NX = 4
SLOTS = 9
KB = 12
LIMIT = 448.0
EPSILON = 1e-06
INV_ROOT = HD ** (-0.5)
EXP2_SCALE = INV_ROOT * math.log2(math.e)
MESH = pl.DeviceIdType.MESH


def seq_of(z_lo, y, core):
    return (z_lo * NY + y) * 2 + core


def place():
    seq = lax.axis_index("seq")
    head = lax.axis_index("head")
    return seq // (2 * NY), (seq // 2) % NY, seq % 2, head // 2, head % 2


def remote(src, dst, send, recv, device):
    return pltpu.make_async_remote_copy(
        src_ref=src,
        dst_ref=dst,
        send_sem=send,
        recv_sem=recv,
        device_id=device,
        device_id_type=MESH,
    )


def greet(devices):
    barrier = pltpu.get_barrier_semaphore()
    for device, valid in devices:
        if valid is None:
            pl.semaphore_signal(barrier, inc=1, device_id=device, device_id_type=MESH)
        else:

            @pl.when(valid)
            def _():
                pl.semaphore_signal(barrier, inc=1, device_id=device, device_id_type=MESH)

    count = jnp.int32(sum(valid is None for _, valid in devices))
    for _, valid in devices:
        if valid is not None:
            count = count + valid.astype(jnp.int32)
    pl.semaphore_wait(barrier, count)


def project_kernel(
    x_hbm, w_hbm, shift_ref, scale_ref, hist_ref,
    qkv_ref, peak_ref,
    xf, wf, rel, quant,
    local_sem, leg_s, leg_r, part_r, xs, xr, zs, zr, ys, yr, yos, yor, cs, cr,
):
    z_lo, y, core, x, z_hi = place()
    seq = seq_of(z_lo, y, core)
    head = x * 2 + z_hi
    rows = xf.shape[1]
    half = rows // 2
    z = z_hi * NZ + z_lo

    def ring_z(step):
        far = (z + step + 2 * NZ) % (2 * NZ)
        return (seq_of(far % NZ, y, core), x * 2 + far // NZ)

    def line_z(step):
        return (seq_of(z_lo + step, y, core), head)

    def ring_y(step):
        return (seq_of(z_lo, (y + step + NY) % NY, core), head)

    def ring_x(step):
        return (seq, ((x + step + NX) % NX) * 2 + z_hi)

    partner_core = (seq_of(z_lo, y, 1 - core), head)
    ahead, behind = ring_z(4), ring_z(-4)
    greet(
        [
            (ahead, None), (behind, None),
            (ring_x(1), None), (ring_x(-1), None),
            (ring_y(1), None), (ring_y(-1), None),
            (partner_core, None),
            (line_z(1), z_lo < NZ - 1), (line_z(-1), z_lo > 0),
        ]
    )
    own_x = pltpu.make_async_copy(x_hbm, xf.at[head], local_sem.at[0])
    own_x.start()
    own_w = pltpu.make_async_copy(w_hbm, wf.at[:, seq], local_sem.at[1])
    own_w.start()

    def part(ref, which):
        return ref.at[pl.ds(which * half, half)]

    leg_one = [
        remote(part(x_hbm, 0), rel.at[0], leg_s.at[0], leg_r.at[0], ahead),
        remote(part(x_hbm, 1), rel.at[1], leg_s.at[1], leg_r.at[1], behind),
    ]
    for copy in leg_one:
        copy.start()

    def z_copy(far_z, which, direction):
        slot = seq_of(far_z, y, core)
        side = 0 if direction > 0 else 1
        return remote(
            wf.at[which, slot], wf.at[which, slot], zs.at[side, far_z, which], zr.at[far_z, which],
            line_z(direction),
        )

    def y_copy(far_z, direction):
        slot = seq_of(far_z, y, core)
        side = 0 if direction > 0 else 1
        return remote(
            wf.at[:, slot], wf.at[:, slot], ys.at[side, far_z], yr.at[side, far_z], ring_y(direction)
        )

    def y_arrival(far_z, direction):
        slot = seq_of(far_z, (y - direction + NY) % NY, core)
        side = 0 if direction > 0 else 1
        return remote(
            wf.at[:, slot], wf.at[:, slot], ys.at[side, far_z], yr.at[side, far_z], ring_y(direction)
        )

    def y_forward(far_z, direction):
        slot = seq_of(far_z, (y - direction + NY) % NY, core)
        return remote(
            wf.at[:, slot], wf.at[:, slot], yos.at[far_z], yor.at[far_z], ring_y(direction)
        )

    def core_copy(far_z, far_y, order):
        slot = seq_of(far_z, far_y, core)
        return remote(
            wf.at[:, slot], wf.at[:, slot], cs.at[far_z, order], cr.at[far_z, order], partner_core
        )

    def have_shard(far_z):
        y_copy(far_z, 1).start()
        y_copy(far_z, -1).start()
        core_copy(far_z, y, 0).start()

    def y_step(far_z):
        for direction in (1, -1):
            far_y = (y - direction + NY) % NY
            y_arrival(far_z, direction).wait_recv()

            @pl.when(far_z % 2 == (0 if direction > 0 else 1))
            def _():
                y_forward(far_z, direction).start()

            core_copy(far_z, far_y, 1 if direction > 0 else 2).start()

    def opposite_step(far_z):
        far_y = (y + 2) % NY
        slot = seq_of(far_z, far_y, core)
        remote(
            wf.at[:, slot], wf.at[:, slot], yos.at[far_z], yor.at[far_z], ring_y(1)
        ).wait_recv()
        core_copy(far_z, far_y, 3).start()

    def inside(far_z):
        return (far_z >= 0) & (far_z < NZ)

    def z_step(step):
        for direction in (1, -1):
            far_z = z_lo - direction * step

            @pl.when(inside(far_z))
            def _():
                for which in range(3):
                    z_copy(far_z, which, direction).wait_recv()

                    @pl.when(inside(z_lo + direction))
                    def _():
                        z_copy(far_z, which, direction).start()

                have_shard(far_z)

    def each_side(step, act):
        for direction in (1, -1):
            far_z = z_lo - direction * step

            @pl.when(inside(far_z))
            def _():
                act(far_z)

    def x_copy(kind, which, direction):
        chunk = x * 2 + (z_hi if kind == 0 else 1 - z_hi)
        side = 0 if direction > 0 else 1
        ref = part(xf.at[chunk], which)
        return remote(ref, ref, xs.at[kind, which, side], xr.at[kind, which, side], ring_x(direction))

    def x_arrival(kind, which, direction):
        chunk = ((x - direction + NX) % NX) * 2 + (z_hi if kind == 0 else 1 - z_hi)
        side = 0 if direction > 0 else 1
        ref = part(xf.at[chunk], which)
        return remote(ref, ref, xs.at[kind, which, side], xr.at[kind, which, side], ring_x(direction))

    def x_forward(kind, which):
        direction = 1 if which == 0 else -1
        chunk = ((x - direction + NX) % NX) * 2 + (z_hi if kind == 0 else 1 - z_hi)
        ref = part(xf.at[chunk], which)
        return remote(ref, ref, xs.at[kind, which, 2], xr.at[kind, which, 2], ring_x(direction))

    def x_opposite(kind, which):
        direction = 1 if which == 0 else -1
        chunk = ((x + 2) % NX) * 2 + (z_hi if kind == 0 else 1 - z_hi)
        ref = part(xf.at[chunk], which)
        return remote(ref, ref, xs.at[kind, which, 2], xr.at[kind, which, 2], ring_x(direction))

    own_w.wait()
    for which in range(3):
        for direction in (1, -1):

            @pl.when(inside(z_lo + direction))
            def _():
                z_copy(z_lo, which, direction).start()

    own_x.wait()
    for which in (0, 1):
        for direction in (1, -1):
            x_copy(0, which, direction).start()
    have_shard(z_lo)

    z_step(1)
    far_chunk = x * 2 + (1 - z_hi)
    leg_two = []
    for which, to in ((0, ahead), (1, behind)):
        leg_one[which].wait_recv()
        source = (z - 4 + 2 * NZ) % (2 * NZ) if which == 0 else (z + 4) % (2 * NZ)
        chunk = x * 2 + source // NZ
        copy = remote(
            rel.at[which], part(xf.at[chunk], which), leg_s.at[2 + which], part_r.at[which], to
        )
        copy.start()
        leg_two.append(copy)
    y_step(z_lo)
    z_step(2)
    each_side(1, y_step)
    opposite_step(z_lo)
    for which in (0, 1):
        x_arrival(0, which, 1).wait_recv()
        x_arrival(0, which, -1).wait_recv()
        x_forward(0, which).start()

    def step_loop(step, _):
        z_step(step)
        each_side(step - 1, y_step)
        each_side(step - 2, opposite_step)
        return 0

    lax.fori_loop(3, 5, step_loop, 0)
    for which in (0, 1):
        ref = part(xf.at[far_chunk], which)
        remote(ref, ref, leg_s.at[2 + which], part_r.at[which], ahead).wait_recv()
        for direction in (1, -1):
            x_copy(1, which, direction).start()
    lax.fori_loop(5, 7, step_loop, 0)
    for which in (0, 1):
        x_arrival(1, which, 1).wait_recv()
        x_arrival(1, which, -1).wait_recv()
        x_forward(1, which).start()
    lax.fori_loop(7, 8, step_loop, 0)
    each_side(7, y_step)
    each_side(6, opposite_step)
    for kind in (0, 1):
        for which in (0, 1):
            x_opposite(kind, which).wait_recv()

    peak = jnp.max(hist_ref[...], axis=1, keepdims=True)
    scale_up = LIMIT / peak
    scale_down = peak / LIMIT
    chunks = xf.shape[0]
    width = xf.shape[2]
    features = chunks * width
    block = 32

    def norm_rows(index, largest):
        at = pl.ds(pl.multiple_of(index * block, block), block)
        total = jnp.zeros((block, width), jnp.float32)
        square = jnp.zeros((block, width), jnp.float32)
        for chunk in range(chunks):
            value = xf[chunk, at, :].astype(jnp.float32)
            total = total + value
            square = square + value * value
        mean = jnp.sum(total, axis=1, keepdims=True) * (1.0 / features)
        mean_square = jnp.sum(square, axis=1, keepdims=True) * (1.0 / features)
        inverse = lax.rsqrt(mean_square - mean * mean + EPSILON)
        for chunk in range(chunks):
            value = xf[chunk, at, :].astype(jnp.float32)
            columns = pl.ds(chunk * width, width)
            modulated = (value - mean) * inverse * (1.0 + scale_ref[:, columns]) + shift_ref[:, columns]
            largest = jnp.maximum(largest, jnp.max(jnp.abs(modulated), axis=0, keepdims=True))
            quant[at, columns] = jnp.clip(modulated * scale_up, -LIMIT, LIMIT).astype(jnp.bfloat16)
        return largest

    largest = lax.fori_loop(0, rows // block, norm_rows, jnp.zeros((1, width), jnp.float32))
    peak_ref[...] = jnp.broadcast_to(jnp.max(largest, axis=1, keepdims=True), peak_ref.shape)

    each_side(7, opposite_step)
    def core_arrivals(far_z, _):
        for order in range(4):
            slot = seq_of(far_z, 0, 1 - core)
            remote(
                wf.at[:, slot], wf.at[:, slot], cs.at[far_z, order], cr.at[far_z, order], partner_core
            ).wait_recv()
        return 0

    lax.fori_loop(0, NZ, core_arrivals, 0)
    depth = wf.shape[1] * wf.shape[2]

    def multiply(which, _):
        weight = wf[which].reshape(depth, width)
        product = jnp.dot(quant[...], weight, preferred_element_type=jnp.float32) * scale_down
        for head_here in range(width // HD):
            qkv_ref[which, head_here] = product[:, head_here * HD : (head_here + 1) * HD].astype(
                jnp.bfloat16
            )
        return 0

    lax.fori_loop(0, 3, multiply, 0)

    for copy in leg_one + leg_two:
        copy.wait_send()
    for kind in (0, 1):
        for which in (0, 1):
            x_copy(kind, which, 1).wait_send()
            x_copy(kind, which, -1).wait_send()
            x_forward(kind, which).wait_send()

    def drain(far_z, _):
        for direction in (1, -1):
            y_copy(far_z, direction).wait_send()

            @pl.when(inside(z_lo + direction) & ((z_lo - far_z) * direction >= 0))
            def _():
                for which in range(3):
                    z_copy(far_z, which, direction).wait_send()

        y_forward(far_z, 1).wait_send()
        for order in range(4):
            core_copy(far_z, y, order).wait_send()
        return 0

    lax.fori_loop(0, NZ, drain, 0)


def project(block_input, mod_shift, mod_scale, history, w_qkv):
    rows, width = block_input.shape
    three, depth, _ = w_qkv.shape
    seqs = lax.axis_size("seq")
    heads = lax.axis_size("head")
    dma = pltpu.SemaphoreType.DMA
    any_space = pl.BlockSpec(memory_space=pl.ANY)
    vmem = pl.BlockSpec(memory_space=pltpu.VMEM)
    return pl.pallas_call(
        project_kernel,
        out_shape=(
            jax.ShapeDtypeStruct((three, width // HD, rows, HD), jnp.bfloat16),
            jax.ShapeDtypeStruct((8, 128), jnp.float32),
        ),
        in_specs=[any_space, any_space, vmem, vmem, vmem],
        out_specs=(vmem, vmem),
        scratch_shapes=[
            pltpu.VMEM((heads, rows, width), jnp.bfloat16),
            pltpu.VMEM((three, seqs, depth, width), jnp.bfloat16),
            pltpu.VMEM((2, rows // 2, width), jnp.bfloat16),
            pltpu.VMEM((rows, heads * width), jnp.bfloat16),
            dma((2,)), dma((4,)), dma((2,)), dma((2,)),
            dma((2, 2, 3)), dma((2, 2, 3)),
            dma((2, NZ, 3)), dma((NZ, 3)),
            dma((2, NZ)), dma((2, NZ)),
            dma((NZ,)), dma((NZ,)),
            dma((NZ, 4)), dma((NZ, 4)),
        ],
        compiler_params=pltpu.CompilerParams(collective_id=0, has_side_effects=True),
        name="gather_project",
    )(block_input, w_qkv, mod_shift.reshape(1, -1), mod_scale.reshape(1, -1), history.reshape(1, -1))


def row_device(z_lo, row, head):
    return (z_lo * GRID_H + row, head)


def halo_kernel(qkv_hbm, peak_hbm, win_hbm, peak_ref, near, far, zs, zr, rs, rr, ms, mr, local_sem):
    z_lo, y, core, x, z_hi = place()
    head = x * 2 + z_hi
    row = y * 2 + core
    up, down = row_device(z_lo, row - 1, head), row_device(z_lo, row + 1, head)
    before, after = row_device(z_lo - 1, row, head), row_device(z_lo + 1, row, head)
    has_up, has_down = row > 0, row < GRID_H - 1
    has_before, has_after = z_lo > 0, z_lo < NZ - 1
    peers_row = [row_device(z_lo, (row + k) % GRID_H, head) for k in range(1, GRID_H)]
    peers_z = [row_device((z_lo + k) % NZ, row, head) for k in range(1, NZ)]
    greet([(d, None) for d in peers_row + peers_z])

    own_peak = pltpu.make_async_copy(peak_hbm, near.at[row], local_sem.at[0])
    own_peak.start()

    def max_near(k):
        return remote(
            peak_hbm, near.at[row], ms.at[0, k - 1], mr.at[0, k - 1], peers_row[k - 1]
        )

    def max_far(k):
        return remote(near, far.at[z_lo], ms.at[1, k - 1], mr.at[1, k - 1], peers_z[k - 1])

    frame_slot = (1, 0, 2)

    def z_copy(part, side):
        slot = 2 if side == 0 else 0
        target, at = (before, 1) if side == 0 else (after, 0)
        del slot
        frame = 2 if side == 0 else 0
        return remote(
            qkv_hbm.at[1 + part], win_hbm.at[frame * 3 + 1, part], zs.at[side, part], zr.at[side, part],
            target,
        )

    for part in (0, 1):
        for side, valid in ((0, has_before), (1, has_after)):

            @pl.when(valid)
            def _():
                z_copy(part, side).start()

    def row_copy(frame, part, side):
        target = up if side == 0 else down
        slot = frame * 3 + (2 if side == 0 else 0)
        source = qkv_hbm.at[1 + part] if frame == 1 else win_hbm.at[frame * 3 + 1, part]
        return remote(
            source, win_hbm.at[slot, part], rs.at[frame, part, side], rr.at[frame, part, side], target
        )

    def rows_out(frame, part):
        for side, valid in ((0, has_up), (1, has_down)):

            @pl.when(valid)
            def _():
                row_copy(frame, part, side).start()

    for k in range(1, GRID_H):
        max_near(k).start()
    for part in (0, 1):
        rows_out(1, part)
    own_peak.wait()
    for k in range(1, GRID_H):
        max_near(k).wait_recv()
    for k in range(1, NZ):
        max_far(k).start()
    arrivals = ((2, 0, has_after), (0, 1, has_before))
    for part in (0, 1):
        for frame, side, valid in arrivals:

            @pl.when(valid)
            def _():
                z_copy(part, side).wait_recv()
                rows_out(frame, part)

    for k in range(1, NZ):
        max_far(k).wait_recv()
    own_far = pltpu.make_async_copy(near, far.at[z_lo], local_sem.at[1])
    own_far.start()
    own_far.wait()
    top = jnp.max(jnp.max(far[...], axis=0), axis=0)
    peak_ref[...] = top

    frames = ((1, None), (2, has_after), (0, has_before))
    for frame, valid_frame in frames:
        for side, valid in ((0, has_down), (1, has_up)):
            ok = valid if valid_frame is None else valid & valid_frame

            @pl.when(ok)
            def _():
                for part in (0, 1):
                    row_copy(frame, part, side).wait_recv()

        for side, valid in ((0, has_up), (1, has_down)):
            ok = valid if valid_frame is None else valid & valid_frame

            @pl.when(ok)
            def _():
                for part in (0, 1):
                    row_copy(frame, part, side).wait_send()

    for part in (0, 1):
        for side, valid in ((0, has_before), (1, has_after)):

            @pl.when(valid)
            def _():
                z_copy(part, side).wait_send()

    for k in range(1, GRID_H):
        max_near(k).wait_send()
    for k in range(1, NZ):
        max_far(k).wait_send()


def halo(qkv, peak):
    _, heads, rows, _ = qkv.shape
    dma = pltpu.SemaphoreType.DMA
    any_space = pl.BlockSpec(memory_space=pl.ANY)
    return pl.pallas_call(
        halo_kernel,
        out_shape=(
            jax.ShapeDtypeStruct((SLOTS, 2, heads, rows, HD), jnp.bfloat16),
            jax.ShapeDtypeStruct((8, 128), jnp.float32),
        ),
        in_specs=[any_space, any_space],
        out_specs=(any_space, pl.BlockSpec(memory_space=pltpu.VMEM)),
        scratch_shapes=[
            pltpu.VMEM((GRID_H, 8, 128), jnp.float32),
            pltpu.VMEM((NZ, GRID_H, 8, 128), jnp.float32),
            dma((2, 2)), dma((2, 2)),
            dma((3, 2, 2)), dma((3, 2, 2)),
            dma((2, 7)), dma((2, 7)),
            dma((2,)),
        ],
        compiler_params=pltpu.CompilerParams(collective_id=1, has_side_effects=True),
        name="halo",
    )(qkv, peak)


def attend_kernel(ids_ref, qkv_hbm, win_hbm, grad_ref, out_ref, gq_ref, part_ref, win, query, acc, sems):
    heads = query.shape[0]
    copies = [pltpu.make_async_copy(qkv_hbm.at[0], query, sems.at[0])]
    for slot in range(SLOTS):
        source = qkv_hbm.at[pl.ds(1, 2)] if slot == 4 else win_hbm.at[slot]
        copies.append(pltpu.make_async_copy(source, win.at[slot], sems.at[1 + slot]))
    for copy in copies:
        copy.start()
    for copy in copies:
        copy.wait()
    tiles = query.shape[1]

    def one_head(head, _):
        columns = pl.ds(pl.multiple_of(head * HD, HD), HD)
        acc[...] = jnp.zeros_like(acc)

        def one_tile(tile, _):
            listed = [ids_ref[tile, slot] for slot in range(KB)]
            q = query[head, tile]
            g = grad_ref[tile, :, columns]
            keys = jnp.concatenate([win[i // 3, 0, head, i % 3] for i in listed], axis=0)
            values = jnp.concatenate([win[i // 3, 1, head, i % 3] for i in listed], axis=0)
            scores = lax.dot_general(
                q, keys, (((1,), (1,)), ((), ())), preferred_element_type=jnp.float32
            )
            top = jnp.max(scores, axis=1, keepdims=True)
            weights = jnp.exp2((scores - top) * EXP2_SCALE)
            prob = weights * (1.0 / jnp.sum(weights, axis=1, keepdims=True))
            low = prob.astype(jnp.bfloat16)
            out = jnp.dot(low, values, preferred_element_type=jnp.float32)
            out_ref[tile, :, columns] = out.astype(jnp.bfloat16)
            gprob = lax.dot_general(
                g, values, (((1,), (1,)), ((), ())), preferred_element_type=jnp.float32
            )
            delta = jnp.sum(g.astype(jnp.float32) * out, axis=1, keepdims=True)
            gscore = (prob * (gprob - delta)).astype(jnp.bfloat16)
            gq = jnp.dot(gscore, keys, preferred_element_type=jnp.float32) * INV_ROOT
            gq_ref[tile, :, columns] = gq.astype(jnp.bfloat16)
            gk = lax.dot_general(
                gscore, q, (((0,), (0,)), ((), ())), preferred_element_type=jnp.float32
            )
            gv = lax.dot_general(
                low, g, (((0,), (0,)), ((), ())), preferred_element_type=jnp.float32
            )
            for slot, i in enumerate(listed):
                span = slice(slot * TILE, (slot + 1) * TILE)
                acc[0, i] += gk[span]
                acc[1, i] += gv[span]
            return 0

        lax.fori_loop(0, tiles, one_tile, 0)

        def write(frame, _):
            for row in range(3):
                for tile in range(3):
                    at = (frame * 3 + row) * 3 + tile
                    part_ref[row, frame, 0, head, tile] = (acc[0, at] * INV_ROOT).astype(jnp.bfloat16)
                    part_ref[row, frame, 1, head, tile] = acc[1, at].astype(jnp.bfloat16)
            return 0

        lax.fori_loop(0, 3, write, 0)
        return 0

    lax.fori_loop(0, heads, one_head, 0)


def attend(ids, qkv, win, out_cotangent):
    _, heads, rows, _ = qkv.shape
    tiles = rows // TILE
    width = heads * HD
    any_space = pl.BlockSpec(memory_space=pl.ANY)
    vmem = pl.BlockSpec(memory_space=pltpu.VMEM)
    return pl.pallas_call(
        attend_kernel,
        out_shape=(
            jax.ShapeDtypeStruct((tiles, TILE, width), jnp.bfloat16),
            jax.ShapeDtypeStruct((tiles, TILE, width), jnp.bfloat16),
            jax.ShapeDtypeStruct((3, 3, 2, heads, tiles, TILE, HD), jnp.bfloat16),
        ),
        in_specs=[pl.BlockSpec(memory_space=pltpu.SMEM), any_space, any_space, vmem],
        out_specs=(vmem, vmem, vmem),
        scratch_shapes=[
            pltpu.VMEM((SLOTS, 2, heads, tiles, TILE, HD), jnp.bfloat16),
            pltpu.VMEM((heads, tiles, TILE, HD), jnp.bfloat16),
            pltpu.VMEM((2, SLOTS * tiles, TILE, HD), jnp.float32),
            pltpu.SemaphoreType.DMA((1 + SLOTS,)),
        ],
        name="attend",
    )(
        ids,
        qkv.reshape(3, heads, tiles, TILE, HD),
        win.reshape(SLOTS, 2, heads, tiles, TILE, HD),
        out_cotangent.reshape(tiles, TILE, width),
    )


def return_kernel(part_hbm, out_ref, own, rows_in, zout, zin, local_sem, rs, rr, zs, zr):
    z_lo, y, core, x, z_hi = place()
    head = x * 2 + z_hi
    row = y * 2 + core
    up, down = row_device(z_lo, row - 1, head), row_device(z_lo, row + 1, head)
    before, after = row_device(z_lo - 1, row, head), row_device(z_lo + 1, row, head)
    has_up, has_down = row > 0, row < GRID_H - 1
    has_before, has_after = z_lo > 0, z_lo < NZ - 1
    greet([(up, has_up), (down, has_down), (before, has_before), (after, has_after)])
    mine = pltpu.make_async_copy(part_hbm.at[1], own, local_sem)
    mine.start()
    frames = ((0, has_before), (2, has_after), (1, None))

    def row_copy(frame, part, side):
        target = up if side == 0 else down
        step = 0 if side == 0 else 2
        return remote(
            part_hbm.at[step, frame, part], rows_in.at[side, frame, part],
            rs.at[frame, part, side], rr.at[frame, part, side], target,
        )

    def both(a, b):
        return a if b is None else a & b

    for part in (0, 1):
        for frame, valid_frame in frames:
            for side, valid in ((0, has_up), (1, has_down)):

                @pl.when(both(valid, valid_frame))
                def _():
                    row_copy(frame, part, side).start()

    @pl.when(jnp.logical_not(has_down))
    def _():
        rows_in[0] = jnp.zeros(rows_in.shape[1:], rows_in.dtype)

    @pl.when(jnp.logical_not(has_up))
    def _():
        rows_in[1] = jnp.zeros(rows_in.shape[1:], rows_in.dtype)

    @pl.when(jnp.logical_not(has_after))
    def _():
        zin[0] = jnp.zeros(zin.shape[1:], zin.dtype)

    @pl.when(jnp.logical_not(has_before))
    def _():
        zin[1] = jnp.zeros(zin.shape[1:], zin.dtype)

    mine.wait()

    def z_copy(part, side):
        target = before if side == 0 else after
        return remote(
            zout.at[side, part], zin.at[side, part], zs.at[side, part], zr.at[side, part], target
        )

    def arrived(frame, part, valid_frame):
        for side, valid in ((0, has_down), (1, has_up)):

            @pl.when(both(valid, valid_frame))
            def _():
                row_copy(frame, part, side).wait_recv()

    def total(frame, part, head_here):
        return (
            own[frame, part, head_here].astype(jnp.float32)
            + rows_in[0, frame, part, head_here].astype(jnp.float32)
            + rows_in[1, frame, part, head_here].astype(jnp.float32)
        )

    heads = own.shape[2]
    for part in (0, 1):
        for frame, side, valid_frame in ((0, 0, has_before), (2, 1, has_after)):
            arrived(frame, part, valid_frame)

            @pl.when(valid_frame)
            def _():
                for head_here in range(heads):
                    zout[side, part, head_here] = total(frame, part, head_here).astype(jnp.bfloat16)
                z_copy(part, side).start()

    for part in (0, 1):
        arrived(1, part, None)
        for side, valid in ((0, has_after), (1, has_before)):

            @pl.when(valid)
            def _():
                z_copy(part, side).wait_recv()

        for head_here in range(heads):
            result = (
                total(1, part, head_here)
                + zin[0, part, head_here].astype(jnp.float32)
                + zin[1, part, head_here].astype(jnp.float32)
            )
            out_ref[part, :, head_here * HD : (head_here + 1) * HD] = result.astype(jnp.bfloat16)

    for part in (0, 1):
        for frame, valid_frame in frames:
            for side, valid in ((0, has_up), (1, has_down)):

                @pl.when(both(valid, valid_frame))
                def _():
                    row_copy(frame, part, side).wait_send()

        for side, valid in ((0, has_before), (1, has_after)):

            @pl.when(valid)
            def _():
                z_copy(part, side).wait_send()


def give_back(parts):
    _, _, _, heads, rows, _ = parts.shape
    dma = pltpu.SemaphoreType.DMA
    half = (2, heads, rows, HD)
    return pl.pallas_call(
        return_kernel,
        out_shape=jax.ShapeDtypeStruct((2, rows, heads * HD), jnp.bfloat16),
        in_specs=[pl.BlockSpec(memory_space=pl.ANY)],
        out_specs=pl.BlockSpec(memory_space=pltpu.VMEM),
        scratch_shapes=[
            pltpu.VMEM((3,) + half, jnp.bfloat16),
            pltpu.VMEM((2, 3) + half, jnp.bfloat16),
            pltpu.VMEM((2,) + half, jnp.bfloat16),
            pltpu.VMEM((2,) + half, jnp.bfloat16),
            dma(()),
            dma((3, 2, 2)), dma((3, 2, 2)),
            dma((2, 2)), dma((2, 2)),
        ],
        compiler_params=pltpu.CompilerParams(collective_id=2, has_side_effects=True),
        name="give_back",
    )(parts)


def local(block_input, mod_shift, mod_scale, history, w_qkv, pattern, out_cotangent):
    rows, width = block_input.shape
    tiles = rows // TILE
    heads = width // HD
    qkv, peak = project(block_input, mod_shift, mod_scale, history, w_qkv)
    win, peak_all = halo(qkv, peak)
    tile_offset = pattern // tiles - lax.axis_index("seq")
    frame_of = (tile_offset + 1) // GRID_H
    slot_of = (frame_of + 1) * 3 + tile_offset - frame_of * GRID_H + 1
    ids = slot_of * tiles + pattern % tiles
    attn_out, grad_query, parts = attend(ids, qkv, win, out_cotangent)
    grad_kv = give_back(parts.reshape(3, 3, 2, heads, rows, HD))
    grad_qkv = jnp.concatenate([grad_query.reshape(1, rows, width), grad_kv], axis=0)
    new_history = jnp.concatenate([peak_all[0, :1], history[:-1]])
    return (attn_out.reshape(rows, width), grad_qkv, new_history)


def solution(mesh):
    placed = (
        P("seq", "head"),
        P(),
        P(),
        P(),
        P(None, "seq", "head"),
        P("seq", None),
        P("seq", "head"),
    )
    return jax.shard_map(
        local,
        mesh=mesh,
        in_specs=placed,
        out_specs=(P("seq", "head"), P(None, "seq", "head"), P()),
        check_vma=False,
    )
```

time: 734 us -> 149 us (0.20); the launches traced: 720 us -> 146 us
  waiting for transfers between devices: 255 us -> 0 us
  blocking collectives: 214 us -> 0 us
  Pallas kernels: 0 us -> 140 us
  local copies, waits for them, and re-layouts: 113 us -> 1.26 us
  matrix products: 54.4 us -> 0 us
  starting transfers between devices: 50.9 us -> 0 us
  between operations: 16.3 us -> 0.7 us
  other arithmetic: 17.4 us -> 4.46 us
    all_gather x2 -> x0, waiting for transfers between devices: 230 us -> none  [the longest x1 121 us: local(): full_weight = lax.all_gather(w_qkv, 'seq', axis=1, tiled=True)]
    pmax x1 -> x0, blocking collectives: 214 us -> none  [local(): abs_peak = lax.pmax(jnp.max(jnp.abs(modulated)), 'seq')]
    pallas_call x0 -> x4, Pallas kernels: none -> 140 us  [the longest x1 77.1 us: project(): pl.pallas_call(project_kernel, out_shape=(jax.ShapeDtypeStruct((three, wi...]
    ppermute x16 -> x0, starting transfers between devices: 50.8 us -> none  [from_behind(): return lax.ppermute(x, axis, pairs)]
    dot_general x24 -> x0, matrix products: 48.4 us -> none  [the longest x3 9.66 us: attend_head(): jnp.einsum('aqwk,aqd->wkd', score_window, query_tile, preferred_element_t...]
    ppermute x16 -> x0, waiting for transfers between devices: 23.6 us -> none  [from_behind(): return lax.ppermute(x, axis, pairs)]
    dot_general x6 -> x0, local copies, waits for them, and re-layouts: 20.2 us -> none  [the longest x3 10.3 us: attend_head(): jnp.einsum('aqsk,asw->aqwk', prob_slots, onehot, preferred_element_type=j...]
    convert_element_type x7 -> x0, local copies, waits for them, and re-layouts: 16.4 us -> none  [the longest x1 11.1 us: local(): partials = lax.optimization_barrier(grad_ext.astype(jnp.bfloat16))]
  transfers between devices with their start and end apart: 18 -> 0, of which waited for: 6 -> 0; matrix products, arithmetic and copies ran while one was open for 4% -> 0% of each run, Pallas kernels for 0% -> 0%
where the time goes in v1:
time: 149 us; the launch traced here: 146 us
  Pallas kernels  140 us (94%)
  other arithmetic  4.46 us (3%)
    pallas_call x1, Pallas kernels, project(): pl.pallas_call(project_kernel, out_shape=(jax.ShapeDtypeStruct((three, wi...  77.1 us
    pallas_call x1, Pallas kernels, give_back(): pl.pallas_call(return_kernel, out_shape=jax.ShapeDtypeStruct((2, rows, he...  23.1 us
    pallas_call x1, Pallas kernels, halo(): pl.pallas_call(halo_kernel, out_shape=(jax.ShapeDtypeStruct((SLOTS, 2, he...  22.8 us
    pallas_call x1, Pallas kernels, attend(): pl.pallas_call(attend_kernel, out_shape=(jax.ShapeDtypeStruct((tiles, TIL...  16.5 us

profile of v1, /device:TPU:1, one launch (start us, length us, event | category | flops | bytes accessed | tf_op | source)
XLA Modules:
  0.0 145.9 jit_solution(9996137458824784519)
XLA Ops:
  0.6 0.0 copy-start.1
  0.6 1.3 fusion.1.ids_ref
  1.9 77.1 %gather_project.1 = (bf16[3,3,288,128]{3,2,1,0:T(8,128)(2,1)}, f32[8,128]{1,0:T(8,128)}) custom-call(bf16[288,384]{1,0:T(8,128)(2,1)} %x_hbm.1, bf16[3,48,384]{2,1,0:T(8,128)(2,1)} %w_hbm.1, f32[1,3072]{1,0:T(1,128)} %bitcast.16, f32[1,3072]{1,0:T(1,128)} %bitcast.17, f32[1,16]{1,0:T(1,128)} %bitcast.18), custom_call_target="tpu_custom_call" | custom-call | tf_op jit(solution)/shard_map/gather_project/pallas_call | solution.py:370
  79.1 22.8 %halo.1 = (bf16[9,2,3,288,128]{4,3,2,1,0:T(8,128)(2,1)}, f32[8,128]{1,0:T(8,128)}) custom-call(bf16[3,3,288,128]{3,2,1,0:T(8,128)(2,1)} %get-tuple-element.10.qkv_hbm, f32[8,128]{1,0:T(8,128)} %get-tuple-element.11.peak_hbm), custom_call_target="tpu_custom_call" | custom-call | tf_op jit(solution)/shard_map/halo/pallas_call | solution.py:517
  101.9 1.2 slice.6
  103.2 16.5 %attend.1 = (bf16[3,96,384]{2,1,0:T(8,128)(2,1)}, bf16[3,96,384]{2,1,0:T(8,128)(2,1)}, bf16[3,3,2,3,3,96,128]{6,5,4,3,2,1,0:T(8,128)(2,1)}) custom-call(s32[3,12]{1,0:T(4,128)} %fusion.1.ids_ref, bf16[3,3,3,96,128]{4,3,2,1,0:T(8,128)(2,1)} %bitcast.13, bf16[9,2,3,3,96,128]{5,4,3,2,1,0:T(8,128)(2,1)} %bitcast.11, bf16[3,96,384]{2,1,0:T(8,128)(2,1)} %bitcast.14), custom_call_target="tpu_custom_call" | custom-call | tf_op jit(solution)/shard_map/attend/pallas_call | solution.py:610
  119.7 0.0 copy-start
  119.7 0.0 copy-done.1
  119.7 1.2 pad_maximum_fusion.1
  120.9 23.1 %give_back.1 = bf16[2,288,384]{2,1,0:T(8,128)(2,1)} custom-call(bf16[3,3,2,3,288,128]{5,4,3,2,1,0:T(8,128)(2,1)} %bitcast.12), custom_call_target="tpu_custom_call" | custom-call | tf_op jit(solution)/shard_map/give_back/pallas_call | solution.py:750
  144.0 0.0 copy-done
  144.0 1.9 %pad_maximum_fusion = bf16[3,288,384]{2,1,0:T(8,128)(2,1)} fusion(bf16[2,288,384]{2,1,0:T(8,128)(2,1)} %give_back.1, bf16[1,288,384]{2,1,0:T(8,128)(2,1)S(1)} %bitcast.15), kind=kLoop, calls=%fused_computation | loop fusion | flops 331776 | bytes 1327104 | tf_op jit(solution)/shard_map/concatenate | solution.py:781
Async XLA Ops:
  0.6 119.1 %copy-start.1 = (f32[16]{0:T(128)S(1)}, f32[16]{0:T(128)}, u32[]{:S(2)}) copy-start(f32[16]{0:T(128)} %param.10) | copy-start | bytes 196
  119.7 24.3 %copy-start = (bf16[3,96,384]{2,1,0:T(8,128)(2,1)S(1)}, bf16[3,96,384]{2,1,0:T(8,128)(2,1)}, u32[]{:S(2)}) copy-start(bf16[3,96,384]{2,1,0:T(8,128)(2,1)} %get-tuple-element.14) | copy-start | bytes 663556

commit v2 on v1

--- a/solution.py
+++ b/solution.py
@@ -396,10 +396,18 @@
     return (z_lo * GRID_H + row, head)
 
 
-def halo_kernel(qkv_hbm, peak_hbm, win_hbm, peak_ref, near, far, zs, zr, rs, rr, ms, mr, local_sem):
+def attention_kernel(
+    pattern_ref, hist_ref, qkv_hbm, peak_hbm, grad_ref,
+    out_ref, gqkv_ref, new_hist_ref,
+    win0, win1, win2, query, gk, gv, parts, rows_in, zout, zin, near, far, ids, slots, repeats,
+    local_sem, zs, zr, rs, rr, ms, mr, bs, br, fs, fr,
+):
     z_lo, y, core, x, z_hi = place()
     head = x * 2 + z_hi
     row = y * 2 + core
+    wins = (win0, win1, win2)
+    heads = len(wins)
+    tiles = query.shape[1]
     up, down = row_device(z_lo, row - 1, head), row_device(z_lo, row + 1, head)
     before, after = row_device(z_lo - 1, row, head), row_device(z_lo + 1, row, head)
     has_up, has_down = row > 0, row < GRID_H - 1
@@ -407,156 +415,177 @@
     peers_row = [row_device(z_lo, (row + k) % GRID_H, head) for k in range(1, GRID_H)]
     peers_z = [row_device((z_lo + k) % NZ, row, head) for k in range(1, NZ)]
     greet([(d, None) for d in peers_row + peers_z])
-
-    own_peak = pltpu.make_async_copy(peak_hbm, near.at[row], local_sem.at[0])
-    own_peak.start()
+    z_sides = ((0, has_before), (1, has_after))
+    row_sides = ((0, has_up), (1, has_down))
+    from_rows = ((0, has_down), (1, has_up))
+    frames = ((0, has_before), (2, has_after), (1, None))
+
+    def both(p, q):
+        return p if q is None else p & q
+
+    def slab(h, slot):
+        return wins[h].at[:, pl.ds(slot * tiles, tiles)]
+
+    def z_copy(h, side):
+        target, frame = (before, 2) if side == 0 else (after, 0)
+        return remote(
+            qkv_hbm.at[pl.ds(1, 2), h], slab(h, frame * 3 + 1), zs.at[h, side], zr.at[h, side], target
+        )
+
+    def row_copy(h, frame, side):
+        target = up if side == 0 else down
+        source = qkv_hbm.at[pl.ds(1, 2), h] if frame == 1 else slab(h, frame * 3 + 1)
+        return remote(
+            source, slab(h, frame * 3 + (2 if side == 0 else 0)),
+            rs.at[h, frame, side], rr.at[h, frame, side], target,
+        )
+
+    def own_slab(h):
+        return pltpu.make_async_copy(qkv_hbm.at[pl.ds(1, 2), h], slab(h, 4), local_sem.at[h])
+
+    def rows_out(h, frame):
+        for side, valid in row_sides:
+
+            @pl.when(valid)
+            def _():
+                row_copy(h, frame, side).start()
+
+    def z_arrive(h):
+        for frame, side, valid in ((2, 0, has_after), (0, 1, has_before)):
+
+            @pl.when(valid)
+            def _():
+                z_copy(h, side).wait_recv()
+                rows_out(h, frame)
+
+    def rows_arrive(h):
+        for frame, valid_frame in frames:
+            for side, valid in from_rows:
+
+                @pl.when(both(valid, valid_frame))
+                def _():
+                    row_copy(h, frame, side).wait_recv()
+
+        own_slab(h).wait()
+
+    own_peak = pltpu.make_async_copy(peak_hbm, near.at[row], local_sem.at[heads])
+    own_far = pltpu.make_async_copy(near, far.at[z_lo], local_sem.at[heads + 1])
+    own_query = pltpu.make_async_copy(qkv_hbm.at[0], query, local_sem.at[heads + 2])
 
     def max_near(k):
-        return remote(
-            peak_hbm, near.at[row], ms.at[0, k - 1], mr.at[0, k - 1], peers_row[k - 1]
-        )
+        return remote(peak_hbm, near.at[row], ms.at[0, k - 1], mr.at[0, k - 1], peers_row[k - 1])
 
     def max_far(k):
         return remote(near, far.at[z_lo], ms.at[1, k - 1], mr.at[1, k - 1], peers_z[k - 1])
 
-    frame_slot = (1, 0, 2)
-
-    def z_copy(part, side):
-        slot = 2 if side == 0 else 0
-        target, at = (before, 1) if side == 0 else (after, 0)
-        del slot
-        frame = 2 if side == 0 else 0
+    def back_row(h, frame, side):
+        target = up if side == 0 else down
         return remote(
-            qkv_hbm.at[1 + part], win_hbm.at[frame * 3 + 1, part], zs.at[side, part], zr.at[side, part],
-            target,
-        )
-
-    for part in (0, 1):
-        for side, valid in ((0, has_before), (1, has_after)):
+            parts.at[h, 0 if side == 0 else 2, frame], rows_in.at[h, side, frame],
+            bs.at[h, frame, side], br.at[h, frame, side], target,
+        )
+
+    def back_z(h, side):
+        target = before if side == 0 else after
+        return remote(zout.at[h, side], zin.at[h, side], fs.at[h, side], fr.at[h, side], target)
+
+    def back_rows_out(h, frame, valid_frame):
+        for side, valid in row_sides:
+
+            @pl.when(both(valid, valid_frame))
+            def _():
+                back_row(h, frame, side).start()
+
+    def back_rows_arrive(h, frame, valid_frame):
+        for side, valid in from_rows:
+
+            @pl.when(both(valid, valid_frame))
+            def _():
+                back_row(h, frame, side).wait_recv()
+
+    own_peak.start()
+    own_query.start()
+    for h in range(heads):
+        own_slab(h).start()
+        for side, valid in z_sides:
 
             @pl.when(valid)
             def _():
-                z_copy(part, side).start()
-
-    def row_copy(frame, part, side):
-        target = up if side == 0 else down
-        slot = frame * 3 + (2 if side == 0 else 0)
-        source = qkv_hbm.at[1 + part] if frame == 1 else win_hbm.at[frame * 3 + 1, part]
-        return remote(
-            source, win_hbm.at[slot, part], rs.at[frame, part, side], rr.at[frame, part, side], target
-        )
-
-    def rows_out(frame, part):
-        for side, valid in ((0, has_up), (1, has_down)):
-
-            @pl.when(valid)
-            def _():
-                row_copy(frame, part, side).start()
-
-    for k in range(1, GRID_H):
-        max_near(k).start()
-    for part in (0, 1):
-        rows_out(1, part)
+                z_copy(h, side).start()
+
+        rows_out(h, 1)
+        if h == 0:
+            for k in range(1, GRID_H):
+                max_near(k).start()
+
+    def clear(buffer, side):
+        for h in range(heads):
+            buffer[h, side] = jnp.zeros(buffer.shape[2:], buffer.dtype)
+
+    for side, valid in from_rows:
+
+        @pl.when(jnp.logical_not(valid))
+        def _():
+            clear(rows_in, side)
+
+    for side, valid in ((0, has_after), (1, has_before)):
+
+        @pl.when(jnp.logical_not(valid))
+        def _():
+            clear(zin, side)
+
+    for tile in range(tiles):
+        gk[tile, KB] = jnp.zeros(gk.shape[2:], gk.dtype)
+        gv[tile, KB] = jnp.zeros(gv.shape[2:], gv.dtype)
+
+    for tile in range(tiles):
+        for slot in range(KB):
+            ids[tile, slot] = 0
+
+    first_slab = (z_lo - 1) * GRID_H + row - 1
+
+    def table(window, _):
+        place_slab = first_slab + (window // 9) * GRID_H + (window // 3) % 3
+        wanted = place_slab * tiles + window % 3
+        for tile in range(tiles):
+            found = jnp.int32(KB)
+            for slot in range(KB):
+                same = pattern_ref[tile, slot] == wanted
+                found = jnp.where(same, slot, found)
+                ids[tile, slot] = jnp.where(same, window, ids[tile, slot])
+            slots[tile, window] = found
+        return 0
+
+    def count(slot, _):
+        for tile in range(tiles):
+            same = [(pattern_ref[tile, slot] == pattern_ref[tile, k]).astype(jnp.int32) for k in range(KB)]
+            repeats[tile, slot] = sum(same).astype(jnp.float32)
+        return 0
+
+    z_arrive(0)
+    lax.fori_loop(0, SLOTS * tiles, table, 0)
+    lax.fori_loop(0, KB, count, 0)
+    z_arrive(1)
     own_peak.wait()
     for k in range(1, GRID_H):
         max_near(k).wait_recv()
+    own_far.start()
     for k in range(1, NZ):
         max_far(k).start()
-    arrivals = ((2, 0, has_after), (0, 1, has_before))
-    for part in (0, 1):
-        for frame, side, valid in arrivals:
-
-            @pl.when(valid)
-            def _():
-                z_copy(part, side).wait_recv()
-                rows_out(frame, part)
-
-    for k in range(1, NZ):
-        max_far(k).wait_recv()
-    own_far = pltpu.make_async_copy(near, far.at[z_lo], local_sem.at[1])
-    own_far.start()
-    own_far.wait()
-    top = jnp.max(jnp.max(far[...], axis=0), axis=0)
-    peak_ref[...] = top
-
-    frames = ((1, None), (2, has_after), (0, has_before))
-    for frame, valid_frame in frames:
-        for side, valid in ((0, has_down), (1, has_up)):
-            ok = valid if valid_frame is None else valid & valid_frame
-
-            @pl.when(ok)
-            def _():
-                for part in (0, 1):
-                    row_copy(frame, part, side).wait_recv()
-
-        for side, valid in ((0, has_up), (1, has_down)):
-            ok = valid if valid_frame is None else valid & valid_frame
-
-            @pl.when(ok)
-            def _():
-                for part in (0, 1):
-                    row_copy(frame, part, side).wait_send()
-
-    for part in (0, 1):
-        for side, valid in ((0, has_before), (1, has_after)):
-
-            @pl.when(valid)
-            def _():
-                z_copy(part, side).wait_send()
-
-    for k in range(1, GRID_H):
-        max_near(k).wait_send()
-    for k in range(1, NZ):
-        max_far(k).wait_send()
-
-
-def halo(qkv, peak):
-    _, heads, rows, _ = qkv.shape
-    dma = pltpu.SemaphoreType.DMA
-    any_space = pl.BlockSpec(memory_space=pl.ANY)
-    return pl.pallas_call(
-        halo_kernel,
-        out_shape=(
-            jax.ShapeDtypeStruct((SLOTS, 2, heads, rows, HD), jnp.bfloat16),
-            jax.ShapeDtypeStruct((8, 128), jnp.float32),
-        ),
-        in_specs=[any_space, any_space],
-        out_specs=(any_space, pl.BlockSpec(memory_space=pltpu.VMEM)),
-        scratch_shapes=[
-            pltpu.VMEM((GRID_H, 8, 128), jnp.float32),
-            pltpu.VMEM((NZ, GRID_H, 8, 128), jnp.float32),
-            dma((2, 2)), dma((2, 2)),
-            dma((3, 2, 2)), dma((3, 2, 2)),
-            dma((2, 7)), dma((2, 7)),
-            dma((2,)),
-        ],
-        compiler_params=pltpu.CompilerParams(collective_id=1, has_side_effects=True),
-        name="halo",
-    )(qkv, peak)
-
-
-def attend_kernel(ids_ref, qkv_hbm, win_hbm, grad_ref, out_ref, gq_ref, part_ref, win, query, acc, sems):
-    heads = query.shape[0]
-    copies = [pltpu.make_async_copy(qkv_hbm.at[0], query, sems.at[0])]
-    for slot in range(SLOTS):
-        source = qkv_hbm.at[pl.ds(1, 2)] if slot == 4 else win_hbm.at[slot]
-        copies.append(pltpu.make_async_copy(source, win.at[slot], sems.at[1 + slot]))
-    for copy in copies:
-        copy.start()
-    for copy in copies:
-        copy.wait()
-    tiles = query.shape[1]
-
-    def one_head(head, _):
-        columns = pl.ds(pl.multiple_of(head * HD, HD), HD)
-        acc[...] = jnp.zeros_like(acc)
+    own_query.wait()
+    rows_arrive(0)
+    z_arrive(2)
+
+    def one_head(h):
+        win = wins[h]
+        columns = slice(h * HD, (h + 1) * HD)
 
         def one_tile(tile, _):
-            listed = [ids_ref[tile, slot] for slot in range(KB)]
-            q = query[head, tile]
+            listed = [ids[tile, slot] for slot in range(KB)]
+            q = query[h, tile]
             g = grad_ref[tile, :, columns]
-            keys = jnp.concatenate([win[i // 3, 0, head, i % 3] for i in listed], axis=0)
-            values = jnp.concatenate([win[i // 3, 1, head, i % 3] for i in listed], axis=0)
+            keys = jnp.concatenate([win[0, i] for i in listed], axis=0)
+            values = jnp.concatenate([win[1, i] for i in listed], axis=0)
             scores = lax.dot_general(
                 q, keys, (((1,), (1,)), ((), ())), preferred_element_type=jnp.float32
             )
@@ -572,215 +601,181 @@
             delta = jnp.sum(g.astype(jnp.float32) * out, axis=1, keepdims=True)
             gscore = (prob * (gprob - delta)).astype(jnp.bfloat16)
             gq = jnp.dot(gscore, keys, preferred_element_type=jnp.float32) * INV_ROOT
-            gq_ref[tile, :, columns] = gq.astype(jnp.bfloat16)
-            gk = lax.dot_general(
+            gqkv_ref[0, tile, :, columns] = gq.astype(jnp.bfloat16)
+            key_terms = lax.dot_general(
                 gscore, q, (((0,), (0,)), ((), ())), preferred_element_type=jnp.float32
             )
-            gv = lax.dot_general(
+            value_terms = lax.dot_general(
                 low, g, (((0,), (0,)), ((), ())), preferred_element_type=jnp.float32
             )
-            for slot, i in enumerate(listed):
+            for slot in range(KB):
                 span = slice(slot * TILE, (slot + 1) * TILE)
-                acc[0, i] += gk[span]
-                acc[1, i] += gv[span]
+                often = repeats[tile, slot]
+                gk[tile, slot] = key_terms[span] * (often * INV_ROOT)
+                gv[tile, slot] = value_terms[span] * often
             return 0
 
         lax.fori_loop(0, tiles, one_tile, 0)
-
-        def write(frame, _):
-            for row in range(3):
-                for tile in range(3):
-                    at = (frame * 3 + row) * 3 + tile
-                    part_ref[row, frame, 0, head, tile] = (acc[0, at] * INV_ROOT).astype(jnp.bfloat16)
-                    part_ref[row, frame, 1, head, tile] = acc[1, at].astype(jnp.bfloat16)
+        waiting = None
+        for frame, valid_frame in frames:
+
+            def gather(at, _):
+                step, column = at // tiles, at % tiles
+                window = frame * 9 + at
+                found = [slots[tile, window] for tile in range(tiles)]
+                key_sum = gk[0, found[0]] + gk[1, found[1]] + gk[2, found[2]]
+                value_sum = gv[0, found[0]] + gv[1, found[1]] + gv[2, found[2]]
+                parts[h, step, frame, 0, column] = key_sum.astype(jnp.bfloat16)
+                parts[h, step, frame, 1, column] = value_sum.astype(jnp.bfloat16)
+                return 0
+
+            lax.fori_loop(0, 3 * tiles, gather, 0)
+            if waiting is not None:
+                back_rows_out(h, *waiting)
+            waiting = (frame, valid_frame)
+        back_rows_out(h, *waiting)
+
+    def total(h, frame, part, tile):
+        return (
+            parts[h, 1, frame, part, tile].astype(jnp.float32)
+            + rows_in[h, 0, frame, part, tile].astype(jnp.float32)
+            + rows_in[h, 1, frame, part, tile].astype(jnp.float32)
+        )
+
+    def reduce_rows(h):
+        for frame, side, valid_frame in ((0, 0, has_before), (2, 1, has_after)):
+
+            @pl.when(valid_frame)
+            def _():
+                back_rows_arrive(h, frame, None)
+
+                def add(at, _):
+                    part, tile = at // tiles, at % tiles
+                    zout[h, side, part, tile] = total(h, frame, part, tile).astype(jnp.bfloat16)
+                    return 0
+
+                lax.fori_loop(0, 2 * tiles, add, 0)
+                back_z(h, side).start()
+
+    def finish(h):
+        back_rows_arrive(h, 1, None)
+        for side, valid in ((0, has_after), (1, has_before)):
+
+            @pl.when(valid)
+            def _():
+                back_z(h, side).wait_recv()
+
+        columns = slice(h * HD, (h + 1) * HD)
+
+        def add(at, _):
+            part, tile = at // tiles, at % tiles
+            result = (
+                total(h, 1, part, tile)
+                + zin[h, 0, part, tile].astype(jnp.float32)
+                + zin[h, 1, part, tile].astype(jnp.float32)
+            )
+            gqkv_ref[1 + part, tile, :, columns] = result.astype(jnp.bfloat16)
             return 0
 
-        lax.fori_loop(0, 3, write, 0)
-        return 0
-
-    lax.fori_loop(0, heads, one_head, 0)
-
-
-def attend(ids, qkv, win, out_cotangent):
+        lax.fori_loop(0, 2 * tiles, add, 0)
+
+    one_head(0)
+    own_far.wait()
+    for k in range(1, NZ):
+        max_far(k).wait_recv()
+    new_hist_ref[0] = jnp.max(far[...])
+    for k in range(1, new_hist_ref.shape[0]):
+        new_hist_ref[k] = hist_ref[k - 1]
+    rows_arrive(1)
+    one_head(1)
+    reduce_rows(0)
+    rows_arrive(2)
+    one_head(2)
+    reduce_rows(1)
+    finish(0)
+    reduce_rows(2)
+    finish(1)
+    finish(2)
+
+    for h in range(heads):
+        for side, valid in z_sides:
+
+            @pl.when(valid)
+            def _():
+                z_copy(h, side).wait_send()
+                back_z(h, side).wait_send()
+
+        for frame, valid_frame in frames:
+            inward = {0: has_before, 2: has_after, 1: None}[frame]
+            for side, valid in row_sides:
+
+                @pl.when(both(valid, inward))
+                def _():
+                    row_copy(h, frame, side).wait_send()
+                    back_row(h, frame, side).wait_send()
+
+    for k in range(1, GRID_H):
+        max_near(k).wait_send()
+    for k in range(1, NZ):
+        max_far(k).wait_send()
+
+
+def attention(pattern, history, qkv, peak, out_cotangent):
     _, heads, rows, _ = qkv.shape
     tiles = rows // TILE
     width = heads * HD
+    dma = pltpu.SemaphoreType.DMA
     any_space = pl.BlockSpec(memory_space=pl.ANY)
     vmem = pl.BlockSpec(memory_space=pltpu.VMEM)
+    smem = pl.BlockSpec(memory_space=pltpu.SMEM)
+    tile = (TILE, HD)
+    slab = (2, tiles) + tile
     return pl.pallas_call(
-        attend_kernel,
+        attention_kernel,
         out_shape=(
             jax.ShapeDtypeStruct((tiles, TILE, width), jnp.bfloat16),
-            jax.ShapeDtypeStruct((tiles, TILE, width), jnp.bfloat16),
-            jax.ShapeDtypeStruct((3, 3, 2, heads, tiles, TILE, HD), jnp.bfloat16),
+            jax.ShapeDtypeStruct((3, tiles, TILE, width), jnp.bfloat16),
+            jax.ShapeDtypeStruct(history.shape, jnp.float32),
         ),
-        in_specs=[pl.BlockSpec(memory_space=pltpu.SMEM), any_space, any_space, vmem],
-        out_specs=(vmem, vmem, vmem),
-        scratch_shapes=[
-            pltpu.VMEM((SLOTS, 2, heads, tiles, TILE, HD), jnp.bfloat16),
-            pltpu.VMEM((heads, tiles, TILE, HD), jnp.bfloat16),
-            pltpu.VMEM((2, SLOTS * tiles, TILE, HD), jnp.float32),
-            pltpu.SemaphoreType.DMA((1 + SLOTS,)),
+        in_specs=[smem, smem, any_space, any_space, vmem],
+        out_specs=(vmem, vmem, smem),
+        scratch_shapes=[pltpu.VMEM((2, SLOTS * tiles) + tile, jnp.bfloat16)] * heads
+        + [
+            pltpu.VMEM((heads, tiles) + tile, jnp.bfloat16),
+            pltpu.VMEM((tiles, KB + 1) + tile, jnp.float32),
+            pltpu.VMEM((tiles, KB + 1) + tile, jnp.float32),
+            pltpu.VMEM((heads, 3, 3) + slab, jnp.bfloat16),
+            pltpu.VMEM((heads, 2, 3) + slab, jnp.bfloat16),
+            pltpu.VMEM((heads, 2) + slab, jnp.bfloat16),
+            pltpu.VMEM((heads, 2) + slab, jnp.bfloat16),
+            pltpu.VMEM((GRID_H, 8, 128), jnp.float32),
+            pltpu.VMEM((NZ, GRID_H, 8, 128), jnp.float32),
+            pltpu.SMEM((tiles, KB), jnp.int32),
+            pltpu.SMEM((tiles, SLOTS * tiles), jnp.int32),
+            pltpu.SMEM((tiles, KB), jnp.float32),
+            dma((heads + 3,)),
+            dma((heads, 2)), dma((heads, 2)),
+            dma((heads, 3, 2)), dma((heads, 3, 2)),
+            dma((2, 7)), dma((2, 7)),
+            dma((heads, 3, 2)), dma((heads, 3, 2)),
+            dma((heads, 2)), dma((heads, 2)),
         ],
-        name="attend",
+        compiler_params=pltpu.CompilerParams(collective_id=1, has_side_effects=True),
+        name="attention",
     )(
-        ids,
+        pattern,
+        history,
         qkv.reshape(3, heads, tiles, TILE, HD),
-        win.reshape(SLOTS, 2, heads, tiles, TILE, HD),
+        peak,
         out_cotangent.reshape(tiles, TILE, width),
     )
 
 
-def return_kernel(part_hbm, out_ref, own, rows_in, zout, zin, local_sem, rs, rr, zs, zr):
-    z_lo, y, core, x, z_hi = place()
-    head = x * 2 + z_hi
-    row = y * 2 + core
-    up, down = row_device(z_lo, row - 1, head), row_device(z_lo, row + 1, head)
-    before, after = row_device(z_lo - 1, row, head), row_device(z_lo + 1, row, head)
-    has_up, has_down = row > 0, row < GRID_H - 1
-    has_before, has_after = z_lo > 0, z_lo < NZ - 1
-    greet([(up, has_up), (down, has_down), (before, has_before), (after, has_after)])
-    mine = pltpu.make_async_copy(part_hbm.at[1], own, local_sem)
-    mine.start()
-    frames = ((0, has_before), (2, has_after), (1, None))
-
-    def row_copy(frame, part, side):
-        target = up if side == 0 else down
-        step = 0 if side == 0 else 2
-        return remote(
-            part_hbm.at[step, frame, part], rows_in.at[side, frame, part],
-            rs.at[frame, part, side], rr.at[frame, part, side], target,
-        )
-
-    def both(a, b):
-        return a if b is None else a & b
-
-    for part in (0, 1):
-        for frame, valid_frame in frames:
-            for side, valid in ((0, has_up), (1, has_down)):
-
-                @pl.when(both(valid, valid_frame))
-                def _():
-                    row_copy(frame, part, side).start()
-
-    @pl.when(jnp.logical_not(has_down))
-    def _():
-        rows_in[0] = jnp.zeros(rows_in.shape[1:], rows_in.dtype)
-
-    @pl.when(jnp.logical_not(has_up))
-    def _():
-        rows_in[1] = jnp.zeros(rows_in.shape[1:], rows_in.dtype)
-
-    @pl.when(jnp.logical_not(has_after))
-    def _():
-        zin[0] = jnp.zeros(zin.shape[1:], zin.dtype)
-
-    @pl.when(jnp.logical_not(has_before))
-    def _():
-        zin[1] = jnp.zeros(zin.shape[1:], zin.dtype)
-
-    mine.wait()
-
-    def z_copy(part, side):
-        target = before if side == 0 else after
-        return remote(
-            zout.at[side, part], zin.at[side, part], zs.at[side, part], zr.at[side, part], target
-        )
-
-    def arrived(frame, part, valid_frame):
-        for side, valid in ((0, has_down), (1, has_up)):
-
-            @pl.when(both(valid, valid_frame))
-            def _():
-                row_copy(frame, part, side).wait_recv()
-
-    def total(frame, part, head_here):
-        return (
-            own[frame, part, head_here].astype(jnp.float32)
-            + rows_in[0, frame, part, head_here].astype(jnp.float32)
-            + rows_in[1, frame, part, head_here].astype(jnp.float32)
-        )
-
-    heads = own.shape[2]
-    for part in (0, 1):
-        for frame, side, valid_frame in ((0, 0, has_before), (2, 1, has_after)):
-            arrived(frame, part, valid_frame)
-
-            @pl.when(valid_frame)
-            def _():
-                for head_here in range(heads):
-                    zout[side, part, head_here] = total(frame, part, head_here).astype(jnp.bfloat16)
-                z_copy(part, side).start()
-
-    for part in (0, 1):
-        arrived(1, part, None)
-        for side, valid in ((0, has_after), (1, has_before)):
-
-            @pl.when(valid)
-            def _():
-                z_copy(part, side).wait_recv()
-
-        for head_here in range(heads):
-            result = (
-                total(1, part, head_here)
-                + zin[0, part, head_here].astype(jnp.float32)
-                + zin[1, part, head_here].astype(jnp.float32)
-            )
-            out_ref[part, :, head_here * HD : (head_here + 1) * HD] = result.astype(jnp.bfloat16)
-
-    for part in (0, 1):
-        for frame, valid_frame in frames:
-            for side, valid in ((0, has_up), (1, has_down)):
-
-                @pl.when(both(valid, valid_frame))
-                def _():
-                    row_copy(frame, part, side).wait_send()
-
-        for side, valid in ((0, has_before), (1, has_after)):
-
-            @pl.when(valid)
-            def _():
-                z_copy(part, side).wait_send()
-
-
-def give_back(parts):
-    _, _, _, heads, rows, _ = parts.shape
-    dma = pltpu.SemaphoreType.DMA
-    half = (2, heads, rows, HD)
-    return pl.pallas_call(
-        return_kernel,
-        out_shape=jax.ShapeDtypeStruct((2, rows, heads * HD), jnp.bfloat16),
-        in_specs=[pl.BlockSpec(memory_space=pl.ANY)],
-        out_specs=pl.BlockSpec(memory_space=pltpu.VMEM),
-        scratch_shapes=[
-            pltpu.VMEM((3,) + half, jnp.bfloat16),
-            pltpu.VMEM((2, 3) + half, jnp.bfloat16),
-            pltpu.VMEM((2,) + half, jnp.bfloat16),
-            pltpu.VMEM((2,) + half, jnp.bfloat16),
-            dma(()),
-            dma((3, 2, 2)), dma((3, 2, 2)),
-            dma((2, 2)), dma((2, 2)),
-        ],
-        compiler_params=pltpu.CompilerParams(collective_id=2, has_side_effects=True),
-        name="give_back",
-    )(parts)
-
-
 def local(block_input, mod_shift, mod_scale, history, w_qkv, pattern, out_cotangent):
     rows, width = block_input.shape
-    tiles = rows // TILE
-    heads = width // HD
     qkv, peak = project(block_input, mod_shift, mod_scale, history, w_qkv)
-    win, peak_all = halo(qkv, peak)
-    tile_offset = pattern // tiles - lax.axis_index("seq")
-    frame_of = (tile_offset + 1) // GRID_H
-    slot_of = (frame_of + 1) * 3 + tile_offset - frame_of * GRID_H + 1
-    ids = slot_of * tiles + pattern % tiles
-    attn_out, grad_query, parts = attend(ids, qkv, win, out_cotangent)
-    grad_kv = give_back(parts.reshape(3, 3, 2, heads, rows, HD))
-    grad_qkv = jnp.concatenate([grad_query.reshape(1, rows, width), grad_kv], axis=0)
-    new_history = jnp.concatenate([peak_all[0, :1], history[:-1]])
-    return (attn_out.reshape(rows, width), grad_qkv, new_history)
+    attn_out, grad_qkv, new_history = attention(pattern, history, qkv, peak, out_cotangent)
+    return (attn_out.reshape(rows, width), grad_qkv.reshape(3, rows, width), new_history)
 
 
 def solution(mesh):

time: 149 us -> 128 us (0.86); the launches traced: 146 us -> 127 us
  Pallas kernels: 140 us -> 122 us
  other arithmetic: 4.46 us -> 0 us
  local copies, waits for them, and re-layouts: 1.26 us -> 4.15 us
    pallas_call x3 -> x1, Pallas kernels: 62.4 us -> 44.7 us  [attention(): pl.pallas_call(attention_kernel, out_shape=(jax.ShapeDtypeStruct((tiles,...]
    unnamed x4 -> x5, local copies, waits for them, and re-layouts: 0.01 us -> 4.15 us
    concatenate x2 -> x0, other arithmetic: 3.18 us -> none  [the longest x1 1.93 us: local(): jnp.concatenate([grad_query.reshape(1, rows, width), grad_kv], axis=0)]
where the time goes in v2:
time: 128 us; the launch traced here: 127 us
  Pallas kernels  122 us (95%)
  local copies, waits for them, and re-layouts  4.15 us (3%)
    pallas_call x1, Pallas kernels, project(): pl.pallas_call(project_kernel, out_shape=(jax.ShapeDtypeStruct((three, wi...  77.1 us
    pallas_call x1, Pallas kernels, attention(): pl.pallas_call(attention_kernel, out_shape=(jax.ShapeDtypeStruct((tiles,...  44.7 us
    unnamed x5, local copies, waits for them, and re-layouts  4.15 us

profile of v2, /device:TPU:1, one launch (start us, length us, event | category | flops | bytes accessed | tf_op | source)
XLA Modules:
  0.0 126.6 jit_solution(12130971470825969999)
XLA Ops:
  0.6 77.1 %gather_project.1 = (bf16[3,3,288,128]{3,2,1,0:T(8,128)(2,1)}, f32[8,128]{1,0:T(8,128)}) custom-call(bf16[288,384]{1,0:T(8,128)(2,1)} %x_hbm.1, bf16[3,48,384]{2,1,0:T(8,128)(2,1)} %w_hbm.1, f32[1,3072]{1,0:T(1,128)} %bitcast.11, f32[1,3072]{1,0:T(1,128)} %bitcast.12, f32[1,16]{1,0:T(1,128)} %bitcast.13), custom_call_target="tpu_custom_call" | custom-call | tf_op jit(solution)/shard_map/gather_project/pallas_call | solution.py:370
  77.7 44.7 %attention.1 = (bf16[3,96,384]{2,1,0:T(8,128)(2,1)}, bf16[3,3,96,384]{3,2,1,0:T(8,128)(2,1)}, f32[16]{0:T(128)}) custom-call(s32[3,12]{1,0:T(4,128)} %pattern_ref.1, f32[16]{0:T(128)} %hist_ref.1, bf16[3,3,3,96,128]{4,3,2,1,0:T(8,128)(2,1)} %bitcast.8, f32[8,128]{1,0:T(8,128)} %get-tuple-element.9.peak_hbm, bf16[3,96,384]{2,1,0:T(8,128)(2,1)} %bitcast.9), custom_call_target="tpu_custom_call" | custom-call | tf_op jit(solution)/shard_map/attention/pallas_call | solution.py:733
  122.5 1.6 %copy.13 = bf16[288,384]{1,0:T(8,128)(2,1)} copy(bf16[288,384]{1,0:T(8,128)(2,1)} %bitcast.10) | data formatting | bytes 442368
  124.1 0.0 copy-start
  124.1 2.0 %copy.14 = bf16[3,288,384]{2,1,0:T(8,128)(2,1)} copy(bf16[3,288,384]{2,1,0:T(8,128)(2,1)} %bitcast.7) | data formatting | bytes 1327104
  126.1 0.0 copy-done
  126.1 0.5 copy.15
Async XLA Ops:
  124.1 2.0 %copy-start = (f32[16]{0:T(128)S(1)}, f32[16]{0:T(128)}, u32[]{:S(2)}) copy-start(f32[16]{0:T(128)} %get-tuple-element.18) | copy-start | bytes 196

commit v3 on v2

v3 whole, which is shorter than its diff:
```python
import functools
import math

import jax
import jax.numpy as jnp
from jax import lax
from jax.experimental import pallas as pl
from jax.experimental.pallas import tpu as pltpu
from jax.sharding import PartitionSpec as P

HD = 128
TILE = 96
GRID_H = 8
NY = 4
NZ = 8
NX = 4
SLOTS = 9
KB = 12
LIMIT = 448.0
EPSILON = 1e-06
INV_ROOT = HD ** (-0.5)
EXP2_SCALE = INV_ROOT * math.log2(math.e)
MESH = pl.DeviceIdType.MESH
PIECES = 6
ORDER = (
    "s0", "s1", "s2", "x", "i0", "k", "i1", "z01", "z11", "i2", "z21", "z02", "a", "i3", "y00", "z12", "y10",
    "z22", "y20", "i4", "z03", "y01", "z13", "y11", "i5", "z23", "y21", "f0", "z04", "y02", "o00", "z14", "y12",
    "o10", "z24", "y22", "f1", "o20", "z05", "y03", "o01", "z15", "y13", "f2", "o11", "z25", "y23", "o21", "n0",
    "z06", "f3", "y04", "o02", "z16", "y14", "o12", "z26", "y24", "n1", "f4", "o22", "z07", "y05", "o03", "z17",
    "y15", "n2", "f5", "o13", "z27", "y25", "o23", "n3", "y06", "o04", "y16", "o14", "y26", "o24", "n4", "y07",
    "o05", "y17", "n5", "o15", "A", "y27", "o25", "o06", "o16", "o26", "o07", "o17", "o27", "c0", "p0", "h0",
    "c1", "p1", "h1", "c2", "p2", "h2", "Z0", "B", "Z1", "R0", "Z2", "C", "t00", "t01", "t02", "g0", "R1", "t10",
    "t11", "t12", "g1", "r0", "R2", "t20", "t21", "t22", "g2", "r1", "F0", "r2", "F1", "D", "F2",
)


def seq_of(z_lo, y, core):
    return (z_lo * NY + y) * 2 + core


def place():
    seq = lax.axis_index("seq")
    head = lax.axis_index("head")
    return seq // (2 * NY), (seq // 2) % NY, seq % 2, head // 2, head % 2


def remote(src, dst, send, recv, device):
    return pltpu.make_async_remote_copy(
        src_ref=src,
        dst_ref=dst,
        send_sem=send,
        recv_sem=recv,
        device_id=device,
        device_id_type=MESH,
    )


def greet(devices):
    barrier = pltpu.get_barrier_semaphore()
    for device, valid in devices:
        if valid is None:
            pl.semaphore_signal(barrier, inc=1, device_id=device, device_id_type=MESH)
        else:

            @pl.when(valid)
            def _():
                pl.semaphore_signal(barrier, inc=1, device_id=device, device_id_type=MESH)

    count = jnp.int32(sum(valid is None for _, valid in devices))
    for _, valid in devices:
        if valid is not None:
            count = count + valid.astype(jnp.int32)
    pl.semaphore_wait(barrier, count)


def row_device(z_lo, row, head):
    return (z_lo * GRID_H + row, head)


def block_kernel(
    pattern_ref, hist_smem, x_hbm, w_hbm, shift_ref, scale_ref, hist_ref, grad_ref,
    out_ref, gqkv_ref, new_hist_ref,
    xf, wf, quant, top, peak_own, qkv,
    win0, win1, win2, gk, gv, parts, rows_in, zout, zin, near, far, ids, slots, repeats,
    own_s, far_s, far_r, xs, xr, ps, pr, wzs, wzr, ys, yr, yos, yor, cs, cr,
    zs, zr, rs, rr, ms, mr, bs, br, fs, fr,
):
    heads = qkv.shape[0]
    z_lo, y, core, x, z_hi = place()
    seq = seq_of(z_lo, y, core)
    head = x * 2 + z_hi
    rows = xf.shape[1]
    piece = rows // PIECES

    def line_z(step):
        return (seq_of(z_lo + step, y, core), head)

    def ring_y(step):
        return (seq_of(z_lo, (y + step + NY) % NY, core), head)

    def ring_x(step):
        return (seq, ((x + step + NX) % NX) * 2 + z_hi)

    partner_core = (seq_of(z_lo, y, 1 - core), head)
    far_half = (seq, x * 2 + 1 - z_hi)
    peers_row = [row_device(z_lo, (y * 2 + core + k) % GRID_H, head) for k in range(1, GRID_H)]
    peers_z = [row_device((z_lo + k) % NZ, y * 2 + core, head) for k in range(1, NZ)]
    greet(
        [(d, None) for d in peers_row + peers_z]
        + [(far_half, None), (ring_x(1), None), (ring_x(-1), None), (ring_x(2), None)]
    )
    own_x = pltpu.make_async_copy(x_hbm, xf.at[head], own_s.at[heads])
    own_x.start()
    own_w = []
    for h in range(heads):
        copy = pltpu.make_async_copy(w_hbm.at[:, :, pl.ds(h * HD, HD)], wf.at[h, seq], own_s.at[h])
        copy.start()
        own_w.append(copy)

    def rows_of(ref, which):
        return ref.at[pl.ds(which * piece, piece)]

    def far_copy(which):
        return remote(
            rows_of(x_hbm, which), rows_of(xf.at[head], which), far_s.at[which], far_r.at[which], far_half
        )

    def far_arrival(which):
        ref = rows_of(xf.at[x * 2 + 1 - z_hi], which)
        return remote(ref, ref, far_s.at[which], far_r.at[which], far_half)

    def w_z(h, far_z, direction):
        ref = wf.at[h, seq_of(far_z, y, core)]
        side = 0 if direction > 0 else 1
        return remote(ref, ref, wzs.at[side, far_z, h], wzr.at[far_z, h], line_z(direction))

    def w_y(h, far_z, direction, arriving):
        source = (y - direction + NY) % NY if arriving else y
        ref = wf.at[h, seq_of(far_z, source, core)]
        side = 0 if direction > 0 else 1
        return remote(ref, ref, ys.at[side, far_z, h], yr.at[side, far_z, h], ring_y(direction))

    def w_opposite(h, far_z, direction):
        ref = wf.at[h, seq_of(far_z, (y - direction + NY) % NY, core)]
        return remote(ref, ref, yos.at[far_z, h], yor.at[far_z, h], ring_y(direction))

    def w_core(h, far_z, far_y, order):
        ref = wf.at[h, seq_of(far_z, far_y, core)]
        return remote(ref, ref, cs.at[far_z, order, h], cr.at[far_z, order, h], partner_core)

    def inside(far_z):
        return (far_z >= 0) & (far_z < NZ)

    def have_shard(h, far_z):
        w_y(h, far_z, 1, False).start()
        w_y(h, far_z, -1, False).start()
        w_core(h, far_z, y, 0).start()

    def each_side(step, act):
        if step == 0:
            act(z_lo)
            return
        for direction in (1, -1):
            far_z = z_lo - direction * step

            @pl.when(inside(far_z))
            def _():
                act(far_z)

    def own_shard(h):
        own_w[h].wait()
        for direction in (1, -1):

            @pl.when(inside(z_lo + direction))
            def _():
                w_z(h, z_lo, direction).start()

        have_shard(h, z_lo)

    def z_step(h, step):
        for direction in (1, -1):
            far_z = z_lo - direction * step

            @pl.when(inside(far_z))
            def _():
                w_z(h, far_z, direction).wait_recv()

                @pl.when(inside(z_lo + direction))
                def _():
                    w_z(h, far_z, direction).start()

                have_shard(h, far_z)

    def y_step(h, step):
        def act(far_z):
            for direction in (1, -1):
                w_y(h, far_z, direction, True).wait_recv()

                @pl.when(far_z % 2 == (0 if direction > 0 else 1))
                def _():
                    w_opposite(h, far_z, direction).start()

                w_core(h, far_z, (y - direction + NY) % NY, 1 if direction > 0 else 2).start()

        each_side(step, act)

    def opposite_step(h, step):
        def act(far_z):
            ref = wf.at[h, seq_of(far_z, (y + 2) % NY, core)]
            remote(ref, ref, yos.at[far_z, h], yor.at[far_z, h], ring_y(1)).wait_recv()
            w_core(h, far_z, (y + 2) % NY, 3).start()

        each_side(step, act)

    def core_step(h):
        def act(far_z, _):
            for order in range(4):
                ref = wf.at[h, seq_of(far_z, 0, 1 - core)]
                remote(
                    ref, ref, cs.at[far_z, order, h], cr.at[far_z, order, h], partner_core
                ).wait_recv()
            return 0

        lax.fori_loop(0, NZ, act, 0)

    steps_x = (1, -1, 2)

    def x_near(order, arriving):
        source = x - steps_x[order] if arriving else x
        ref = xf.at[((source + NX) % NX) * 2 + z_hi]
        return remote(ref, ref, xs.at[order], xr.at[order], ring_x(steps_x[order]))

    def x_far(which, order, arriving):
        source = x - steps_x[order] if arriving else x
        ref = rows_of(xf.at[((source + NX) % NX) * 2 + 1 - z_hi], which)
        return remote(ref, ref, ps.at[which, order], pr.at[which, order], ring_x(steps_x[order]))

    def far_step(which):
        far_arrival(which).wait_recv()
        for order in range(3):
            x_far(which, order, False).start()

    peak = jnp.max(hist_ref[...], axis=1, keepdims=True)
    scale_up = LIMIT / peak
    scale_down = peak / LIMIT
    chunks = xf.shape[0]
    width = xf.shape[2]
    features = chunks * width
    block = 16

    def norm_rows(index, largest):
        at = pl.ds(pl.multiple_of(index * block, block), block)
        total = jnp.zeros((block, width), jnp.float32)
        square = jnp.zeros((block, width), jnp.float32)
        for chunk in range(chunks):
            value = xf[chunk, at, :].astype(jnp.float32)
            total = total + value
            square = square + value * value
        mean = jnp.sum(total, axis=1, keepdims=True) * (1.0 / features)
        mean_square = jnp.sum(square, axis=1, keepdims=True) * (1.0 / features)
        inverse = lax.rsqrt(mean_square - mean * mean + EPSILON)
        for chunk in range(chunks):
            value = xf[chunk, at, :].astype(jnp.float32)
            columns = pl.ds(chunk * width, width)
            modulated = (value - mean) * inverse * (1.0 + scale_ref[:, columns]) + shift_ref[:, columns]
            largest = jnp.maximum(largest, jnp.max(jnp.abs(modulated), axis=0, keepdims=True))
            quant[at, columns] = jnp.clip(modulated * scale_up, -LIMIT, LIMIT).astype(jnp.bfloat16)
        return largest

    def norm_step(which):
        for order in range(3):
            x_far(which, order, True).wait_recv()
        per = piece // block
        top[...] = lax.fori_loop(which * per, (which + 1) * per, norm_rows, top[...])

    def near_step():
        for order in range(3):
            x_near(order, True).wait_recv()

    def near_out():
        own_x.wait()
        for order in range(3):
            x_near(order, False).start()

    def project(h):
        depth = wf.shape[1] * wf.shape[3]
        for which in range(3):
            weight = wf[h, :, which].reshape(depth, HD)
            product = jnp.dot(quant[...], weight, preferred_element_type=jnp.float32) * scale_down
            qkv[h, which] = product.astype(jnp.bfloat16).reshape(qkv.shape[2:])

    row = y * 2 + core
    wins = (win0, win1, win2)
    tiles = qkv.shape[2]
    up, down = row_device(z_lo, row - 1, head), row_device(z_lo, row + 1, head)
    before, after = row_device(z_lo - 1, row, head), row_device(z_lo + 1, row, head)
    has_up, has_down = row > 0, row < GRID_H - 1
    has_before, has_after = z_lo > 0, z_lo < NZ - 1
    z_sides = ((0, has_before), (1, has_after))
    row_sides = ((0, has_up), (1, has_down))
    from_rows = ((0, has_down), (1, has_up))
    frames = ((0, has_before), (2, has_after), (1, None))

    def both(p, q):
        return p if q is None else p & q

    def slab(h, slot):
        return wins[h].at[:, pl.ds(slot * tiles, tiles)]

    def z_copy(h, side):
        target, frame = (before, 2) if side == 0 else (after, 0)
        return remote(
            qkv.at[h, pl.ds(1, 2)], slab(h, frame * 3 + 1), zs.at[h, side], zr.at[h, side], target
        )

    def row_copy(h, frame, side):
        target = up if side == 0 else down
        source = qkv.at[h, pl.ds(1, 2)] if frame == 1 else slab(h, frame * 3 + 1)
        return remote(
            source, slab(h, frame * 3 + (2 if side == 0 else 0)),
            rs.at[h, frame, side], rr.at[h, frame, side], target,
        )

    def own_slab(h):
        return pltpu.make_async_copy(qkv.at[h, pl.ds(1, 2)], slab(h, 4), own_s.at[heads + 1 + h])

    def rows_out(h, frame):
        for side, valid in row_sides:

            @pl.when(valid)
            def _():
                row_copy(h, frame, side).start()

    def z_arrive(h):
        for frame, side, valid in ((2, 0, has_after), (0, 1, has_before)):

            @pl.when(valid)
            def _():
                z_copy(h, side).wait_recv()
                rows_out(h, frame)

    def rows_arrive(h):
        for frame, valid_frame in frames:
            for side, valid in from_rows:

                @pl.when(both(valid, valid_frame))
                def _():
                    row_copy(h, frame, side).wait_recv()

        own_slab(h).wait()

    own_peak = pltpu.make_async_copy(peak_own, near.at[row], own_s.at[2 * heads + 1])
    own_far = pltpu.make_async_copy(near, far.at[z_lo], own_s.at[2 * heads + 2])
    def max_near(k):
        return remote(peak_own, near.at[row], ms.at[0, k - 1], mr.at[0, k - 1], peers_row[k - 1])

    def max_far(k):
        return remote(near, far.at[z_lo], ms.at[1, k - 1], mr.at[1, k - 1], peers_z[k - 1])

    def back_row(h, frame, side):
        target = up if side == 0 else down
        return remote(
            parts.at[h, 0 if side == 0 else 2, frame], rows_in.at[h, side, frame],
            bs.at[h, frame, side], br.at[h, frame, side], target,
        )

    def back_z(h, side):
        target = before if side == 0 else after
        return remote(zout.at[h, side], zin.at[h, side], fs.at[h, side], fr.at[h, side], target)

    def back_rows_out(h, frame, valid_frame):
        for side, valid in row_sides:

            @pl.when(both(valid, valid_frame))
            def _():
                back_row(h, frame, side).start()

    def back_rows_arrive(h, frame, valid_frame):
        for side, valid in from_rows:

            @pl.when(both(valid, valid_frame))
            def _():
                back_row(h, frame, side).wait_recv()

    def halo_out(h):
        own_slab(h).start()
        for side, valid in z_sides:

            @pl.when(valid)
            def _():
                z_copy(h, side).start()

        rows_out(h, 1)

    def max_one():
        peak_own[...] = jnp.broadcast_to(jnp.max(top[...], axis=1, keepdims=True), peak_own.shape)

    def max_two():
        own_peak.start()
        for k in range(1, GRID_H):
            max_near(k).start()

    def max_three():
        own_peak.wait()
        for k in range(1, GRID_H):
            max_near(k).wait_recv()
        own_far.start()
        for k in range(1, NZ):
            max_far(k).start()

    def max_four():
        own_far.wait()
        for k in range(1, NZ):
            max_far(k).wait_recv()
        new_hist_ref[0] = jnp.max(far[...])
        for k in range(1, new_hist_ref.shape[0]):
            new_hist_ref[k] = hist_smem[k - 1]

    def prepare():
        def clear(buffer, side):
            for h in range(heads):
                buffer[h, side] = jnp.zeros(buffer.shape[2:], buffer.dtype)

        for side, valid in from_rows:

            @pl.when(jnp.logical_not(valid))
            def _():
                clear(rows_in, side)

        for side, valid in ((0, has_after), (1, has_before)):

            @pl.when(jnp.logical_not(valid))
            def _():
                clear(zin, side)

        for tile in range(tiles):
            gk[tile, KB] = jnp.zeros(gk.shape[2:], gk.dtype)
            gv[tile, KB] = jnp.zeros(gv.shape[2:], gv.dtype)

        for tile in range(tiles):
            for slot in range(KB):
                ids[tile, slot] = 0

        first_slab = (z_lo - 1) * GRID_H + row - 1

        def table(window, _):
            place_slab = first_slab + (window // 9) * GRID_H + (window // 3) % 3
            wanted = place_slab * tiles + window % 3
            for tile in range(tiles):
                found = jnp.int32(KB)
                for slot in range(KB):
                    same = pattern_ref[tile, slot] == wanted
                    found = jnp.where(same, slot, found)
                    ids[tile, slot] = jnp.where(same, window, ids[tile, slot])
                slots[tile, window] = found
            return 0

        def count(slot, _):
            for tile in range(tiles):
                same = [(pattern_ref[tile, slot] == pattern_ref[tile, k]).astype(jnp.int32) for k in range(KB)]
                repeats[tile, slot] = sum(same).astype(jnp.float32)
            return 0

        lax.fori_loop(0, SLOTS * tiles, table, 0)
        lax.fori_loop(0, KB, count, 0)

    def attend(h, tile):
        win = wins[h]
        columns = slice(h * HD, (h + 1) * HD)
        listed = [ids[tile, slot] for slot in range(KB)]
        q = qkv[h, 0, tile]
        g = grad_ref[tile, :, columns]
        keys = jnp.concatenate([win[0, i] for i in listed], axis=0)
        values = jnp.concatenate([win[1, i] for i in listed], axis=0)
        scores = lax.dot_general(
            q, keys, (((1,), (1,)), ((), ())), preferred_element_type=jnp.float32
        )
        top = jnp.max(scores, axis=1, keepdims=True)
        weights = jnp.exp2((scores - top) * EXP2_SCALE)
        prob = weights * (1.0 / jnp.sum(weights, axis=1, keepdims=True))
        low = prob.astype(jnp.bfloat16)
        out = jnp.dot(low, values, preferred_element_type=jnp.float32)
        out_ref[tile, :, columns] = out.astype(jnp.bfloat16)
        gprob = lax.dot_general(
            g, values, (((1,), (1,)), ((), ())), preferred_element_type=jnp.float32
        )
        delta = jnp.sum(g.astype(jnp.float32) * out, axis=1, keepdims=True)
        gscore = (prob * (gprob - delta)).astype(jnp.bfloat16)
        gq = jnp.dot(gscore, keys, preferred_element_type=jnp.float32) * INV_ROOT
        gqkv_ref[0, tile, :, columns] = gq.astype(jnp.bfloat16)
        key_terms = lax.dot_general(
            gscore, q, (((0,), (0,)), ((), ())), preferred_element_type=jnp.float32
        )
        value_terms = lax.dot_general(
            low, g, (((0,), (0,)), ((), ())), preferred_element_type=jnp.float32
        )
        for slot in range(KB):
            span = slice(slot * TILE, (slot + 1) * TILE)
            often = repeats[tile, slot]
            gk[tile, slot] = key_terms[span] * (often * INV_ROOT)
            gv[tile, slot] = value_terms[span] * often
    def give_back(h):
        waiting = None
        for frame, valid_frame in frames:

            def gather(at, _):
                step, column = at // tiles, at % tiles
                window = frame * 9 + at
                found = [slots[tile, window] for tile in range(tiles)]
                key_sum = gk[0, found[0]] + gk[1, found[1]] + gk[2, found[2]]
                value_sum = gv[0, found[0]] + gv[1, found[1]] + gv[2, found[2]]
                parts[h, step, frame, 0, column] = key_sum.astype(jnp.bfloat16)
                parts[h, step, frame, 1, column] = value_sum.astype(jnp.bfloat16)
                return 0

            lax.fori_loop(0, 3 * tiles, gather, 0)
            if waiting is not None:
                back_rows_out(h, *waiting)
            waiting = (frame, valid_frame)
        back_rows_out(h, *waiting)

    def total(h, frame, part, tile):
        return (
            parts[h, 1, frame, part, tile].astype(jnp.float32)
            + rows_in[h, 0, frame, part, tile].astype(jnp.float32)
            + rows_in[h, 1, frame, part, tile].astype(jnp.float32)
        )

    def reduce_rows(h):
        for frame, side, valid_frame in ((0, 0, has_before), (2, 1, has_after)):

            @pl.when(valid_frame)
            def _():
                back_rows_arrive(h, frame, None)

                def add(at, _):
                    part, tile = at // tiles, at % tiles
                    zout[h, side, part, tile] = total(h, frame, part, tile).astype(jnp.bfloat16)
                    return 0

                lax.fori_loop(0, 2 * tiles, add, 0)
                back_z(h, side).start()

    def finish(h):
        back_rows_arrive(h, 1, None)
        for side, valid in ((0, has_after), (1, has_before)):

            @pl.when(valid)
            def _():
                back_z(h, side).wait_recv()

        columns = slice(h * HD, (h + 1) * HD)

        def add(at, _):
            part, tile = at // tiles, at % tiles
            result = (
                total(h, 1, part, tile)
                + zin[h, 0, part, tile].astype(jnp.float32)
                + zin[h, 1, part, tile].astype(jnp.float32)
            )
            gqkv_ref[1 + part, tile, :, columns] = result.astype(jnp.bfloat16)
            return 0

        lax.fori_loop(0, 2 * tiles, add, 0)

    acts = {
        "s": own_shard,
        "z": z_step,
        "y": y_step,
        "o": opposite_step,
        "c": core_step,
        "p": project,
        "x": near_out,
        "a": near_step,
        "i": lambda which: far_copy(which).start(),
        "f": far_step,
        "n": norm_step,
        "h": halo_out,
        "Z": z_arrive,
        "R": rows_arrive,
        "t": attend,
        "g": give_back,
        "r": reduce_rows,
        "F": finish,
        "k": prepare,
        "A": max_one,
        "B": max_two,
        "C": max_three,
        "D": max_four,
    }
    top[...] = jnp.zeros_like(top)
    for item in ORDER:
        acts[item[0]](*[int(digit) for digit in item[1:]])

    for order in range(3):
        x_near(order, False).wait_send()
    for which in range(PIECES):
        far_copy(which).wait_send()
        for order in range(3):
            x_far(which, order, False).wait_send()

    def drain(far_z, _):
        for h in range(heads):
            for direction in (1, -1):
                w_y(h, far_z, direction, False).wait_send()

                @pl.when(inside(z_lo + direction) & ((z_lo - far_z) * direction >= 0))
                def _():
                    w_z(h, far_z, direction).wait_send()

            w_opposite(h, far_z, 1).wait_send()
            for order in range(4):
                w_core(h, far_z, y, order).wait_send()
        return 0

    lax.fori_loop(0, NZ, drain, 0)
    for h in range(heads):
        for side, valid in z_sides:

            @pl.when(valid)
            def _():
                z_copy(h, side).wait_send()
                back_z(h, side).wait_send()

        for frame, valid_frame in frames:
            inward = {0: has_before, 2: has_after, 1: None}[frame]
            for side, valid in row_sides:

                @pl.when(both(valid, inward))
                def _():
                    row_copy(h, frame, side).wait_send()
                    back_row(h, frame, side).wait_send()

    for k in range(1, GRID_H):
        max_near(k).wait_send()
    for k in range(1, NZ):
        max_far(k).wait_send()


def local(block_input, mod_shift, mod_scale, history, w_qkv, pattern, out_cotangent):
    rows, width = block_input.shape
    three, depth, _ = w_qkv.shape
    seqs = lax.axis_size("seq")
    chunks = lax.axis_size("head")
    heads = width // HD
    tiles = rows // TILE
    dma = pltpu.SemaphoreType.DMA
    any_space = pl.BlockSpec(memory_space=pl.ANY)
    vmem = pl.BlockSpec(memory_space=pltpu.VMEM)
    smem = pl.BlockSpec(memory_space=pltpu.SMEM)
    tile = (TILE, HD)
    slab = (2, tiles) + tile
    attn_out, grad_qkv, new_history = pl.pallas_call(
        block_kernel,
        out_shape=(
            jax.ShapeDtypeStruct((tiles, TILE, width), jnp.bfloat16),
            jax.ShapeDtypeStruct((3, tiles, TILE, width), jnp.bfloat16),
            jax.ShapeDtypeStruct(history.shape, jnp.float32),
        ),
        in_specs=[smem, smem, any_space, any_space, vmem, vmem, vmem, vmem],
        out_specs=(vmem, vmem, smem),
        scratch_shapes=[
            pltpu.VMEM((chunks, rows, width), jnp.bfloat16),
            pltpu.VMEM((heads, seqs, three, depth, HD), jnp.bfloat16),
            pltpu.VMEM((rows, chunks * width), jnp.bfloat16),
            pltpu.VMEM((1, width), jnp.float32),
            pltpu.VMEM((8, 128), jnp.float32),
            pltpu.VMEM((heads, 3, tiles) + tile, jnp.bfloat16),
        ]
        + [pltpu.VMEM((2, SLOTS * tiles) + tile, jnp.bfloat16)] * heads
        + [
            pltpu.VMEM((tiles, KB + 1) + tile, jnp.float32),
            pltpu.VMEM((tiles, KB + 1) + tile, jnp.float32),
            pltpu.VMEM((heads, 3, 3) + slab, jnp.bfloat16),
            pltpu.VMEM((heads, 2, 3) + slab, jnp.bfloat16),
            pltpu.VMEM((heads, 2) + slab, jnp.bfloat16),
            pltpu.VMEM((heads, 2) + slab, jnp.bfloat16),
            pltpu.VMEM((GRID_H, 8, 128), jnp.float32),
            pltpu.VMEM((NZ, GRID_H, 8, 128), jnp.float32),
            pltpu.SMEM((tiles, KB), jnp.int32),
            pltpu.SMEM((tiles, SLOTS * tiles), jnp.int32),
            pltpu.SMEM((tiles, KB), jnp.float32),
            dma((2 * heads + 3,)), dma((PIECES,)), dma((PIECES,)),
            dma((3,)), dma((3,)),
            dma((PIECES, 3)), dma((PIECES, 3)),
            dma((2, NZ, heads)), dma((NZ, heads)),
            dma((2, NZ, heads)), dma((2, NZ, heads)),
            dma((NZ, heads)), dma((NZ, heads)),
            dma((NZ, 4, heads)), dma((NZ, 4, heads)),
            dma((heads, 2)), dma((heads, 2)),
            dma((heads, 3, 2)), dma((heads, 3, 2)),
            dma((2, 7)), dma((2, 7)),
            dma((heads, 3, 2)), dma((heads, 3, 2)),
            dma((heads, 2)), dma((heads, 2)),
        ],
        compiler_params=pltpu.CompilerParams(collective_id=0, has_side_effects=True),
        name="block",
    )(
        pattern,
        history,
        block_input,
        w_qkv,
        mod_shift.reshape(1, -1),
        mod_scale.reshape(1, -1),
        history.reshape(1, -1),
        out_cotangent.reshape(tiles, TILE, width),
    )
    return (attn_out.reshape(rows, width), grad_qkv.reshape(3, rows, width), new_history)


def solution(mesh):
    placed = (
        P("seq", "head"),
        P(),
        P(),
        P(),
        P(None, "seq", "head"),
        P("seq", None),
        P("seq", "head"),
    )
    return jax.shard_map(
        local,
        mesh=mesh,
        in_specs=placed,
        out_specs=(P("seq", "head"), P(None, "seq", "head"), P()),
        check_vma=False,
    )
```

time: 128 us -> 113 us (0.88)
  Pallas kernels: 122 us -> 108 us
    pallas_call x2 -> x1, Pallas kernels: 122 us -> 108 us  [local(): pl.pallas_call(block_kernel, out_shape=(jax.ShapeDtypeStruct((tiles, TILE...]
where the time goes in v3:
time: 113 us; the launch traced here: 112 us
  Pallas kernels  108 us (96%)
  local copies, waits for them, and re-layouts  4.15 us (4%)
    pallas_call x1, Pallas kernels, local(): pl.pallas_call(block_kernel, out_shape=(jax.ShapeDtypeStruct((tiles, TILE...  108 us
    unnamed x5, local copies, waits for them, and re-layouts  4.15 us

profile of v3, /device:TPU:1, one launch (start us, length us, event | category | flops | bytes accessed | tf_op | source)
XLA Modules:
  0.0 112.3 jit_solution(16006182421894459898)
XLA Ops:
  0.6 107.5 %block.1 = (bf16[3,96,384]{2,1,0:T(8,128)(2,1)}, bf16[3,3,96,384]{3,2,1,0:T(8,128)(2,1)}, f32[16]{0:T(128)}) custom-call(s32[3,12]{1,0:T(4,128)} %pattern_ref.1, f32[16]{0:T(128)} %hist_smem.1, bf16[288,384]{1,0:T(8,128)(2,1)} %x_hbm.1, bf16[3,48,384]{2,1,0:T(8,128)(2,1)} %w_hbm.1, f32[1,3072]{1,0:T(1,128)} %bitcast.9, f32[1,3072]{1,0:T(1,128)} %bitcast.10, ...), custom_call_target="tpu_custom_call" | custom-call | tf_op jit(solution)/shard_map/block/pallas_call | solution.py:653
  108.2 1.6 %copy.13 = bf16[288,384]{1,0:T(8,128)(2,1)} copy(bf16[288,384]{1,0:T(8,128)(2,1)} %bitcast.8) | data formatting | bytes 442368
  109.8 0.0 copy-start
  109.8 2.0 %copy.14 = bf16[3,288,384]{2,1,0:T(8,128)(2,1)} copy(bf16[3,288,384]{2,1,0:T(8,128)(2,1)} %bitcast.6) | data formatting | bytes 1327104
  111.8 0.0 copy-done
  111.8 0.5 copy.15
Async XLA Ops:
  109.8 2.0 %copy-start = (f32[16]{0:T(128)S(1)}, f32[16]{0:T(128)}, u32[]{:S(2)}) copy-start(f32[16]{0:T(128)} %get-tuple-element.14) | copy-start | bytes 196

commit v4 on v3

--- a/solution.py
+++ b/solution.py
@@ -30,7 +30,7 @@
     "y15", "n2", "f5", "o13", "z27", "y25", "o23", "n3", "y06", "o04", "y16", "o14", "y26", "o24", "n4", "y07",
     "o05", "y17", "n5", "o15", "A", "y27", "o25", "o06", "o16", "o26", "o07", "o17", "o27", "c0", "p0", "h0",
     "c1", "p1", "h1", "c2", "p2", "h2", "Z0", "B", "Z1", "R0", "Z2", "C", "t00", "t01", "t02", "g0", "R1", "t10",
-    "t11", "t12", "g1", "r0", "R2", "t20", "t21", "t22", "g2", "r1", "F0", "r2", "F1", "D", "F2",
+    "t11", "t12", "g1", "r0", "R2", "t20", "t21", "r1", "t22", "g2", "F0", "r2", "F1", "D", "F2",
 )
 
 

time: 113 us -> 115 us (1.018)
    pallas_call x1, Pallas kernels: 108 us -> 109 us  [local(): pl.pallas_call(block_kernel, out_shape=(jax.ShapeDtypeStruct((tiles, TILE...]
where the time goes in v4:
time: 115 us; the launch traced here: 114 us
  Pallas kernels  109 us (95%)
  local copies, waits for them, and re-layouts  4.15 us (4%)
    pallas_call x1, Pallas kernels, local(): pl.pallas_call(block_kernel, out_shape=(jax.ShapeDtypeStruct((tiles, TILE...  109 us
    unnamed x5, local copies, waits for them, and re-layouts  4.15 us

profile of v4, /device:TPU:1, one launch (start us, length us, event | category | flops | bytes accessed | tf_op | source)
XLA Modules:
  0.0 114.0 jit_solution(9798228211455360233)
XLA Ops:
  0.6 109.2 %block.1 = (bf16[3,96,384]{2,1,0:T(8,128)(2,1)}, bf16[3,3,96,384]{3,2,1,0:T(8,128)(2,1)}, f32[16]{0:T(128)}) custom-call(s32[3,12]{1,0:T(4,128)} %pattern_ref.1, f32[16]{0:T(128)} %hist_smem.1, bf16[288,384]{1,0:T(8,128)(2,1)} %x_hbm.1, bf16[3,48,384]{2,1,0:T(8,128)(2,1)} %w_hbm.1, f32[1,3072]{1,0:T(1,128)} %bitcast.9, f32[1,3072]{1,0:T(1,128)} %bitcast.10, ...), custom_call_target="tpu_custom_call" | custom-call | tf_op jit(solution)/shard_map/block/pallas_call | solution.py:653
  109.8 1.6 %copy.13 = bf16[288,384]{1,0:T(8,128)(2,1)} copy(bf16[288,384]{1,0:T(8,128)(2,1)} %bitcast.8) | data formatting | bytes 442368
  111.5 0.0 copy-start
  111.5 2.0 %copy.14 = bf16[3,288,384]{2,1,0:T(8,128)(2,1)} copy(bf16[3,288,384]{2,1,0:T(8,128)(2,1)} %bitcast.6) | data formatting | bytes 1327104
  113.5 0.0 copy-done
  113.5 0.5 copy.15
Async XLA Ops:
  111.5 2.0 %copy-start = (f32[16]{0:T(128)S(1)}, f32[16]{0:T(128)}, u32[]{:S(2)}) copy-start(f32[16]{0:T(128)} %get-tuple-element.14) | copy-start | bytes 196

commit v5 on v3

--- a/solution.py
+++ b/solution.py
@@ -23,12 +23,12 @@
 MESH = pl.DeviceIdType.MESH
 PIECES = 6
 ORDER = (
-    "s0", "s1", "s2", "x", "i0", "k", "i1", "z01", "z11", "i2", "z21", "z02", "a", "i3", "y00", "z12", "y10",
-    "z22", "y20", "i4", "z03", "y01", "z13", "y11", "i5", "z23", "y21", "f0", "z04", "y02", "o00", "z14", "y12",
-    "o10", "z24", "y22", "f1", "o20", "z05", "y03", "o01", "z15", "y13", "f2", "o11", "z25", "y23", "o21", "n0",
-    "z06", "f3", "y04", "o02", "z16", "y14", "o12", "z26", "y24", "n1", "f4", "o22", "z07", "y05", "o03", "z17",
-    "y15", "n2", "f5", "o13", "z27", "y25", "o23", "n3", "y06", "o04", "y16", "o14", "y26", "o24", "n4", "y07",
-    "o05", "y17", "n5", "o15", "A", "y27", "o25", "o06", "o16", "o26", "o07", "o17", "o27", "c0", "p0", "h0",
+    "s0", "s1", "s2", "x", "i0", "k", "i1", "i2", "z01", "z11", "i3", "z21", "i4", "z02", "a", "y00", "z12",
+    "y10", "i5", "z22", "y20", "z03", "y01", "z13", "y11", "z23", "y21", "f0", "z04", "y02", "o00", "z14", "y12",
+    "f1", "o10", "z24", "y22", "o20", "f2", "z05", "y03", "o01", "z15", "y13", "f3", "o11", "z25", "y23", "o21",
+    "n0", "f4", "z06", "y04", "o02", "z16", "y14", "n1", "f5", "o12", "z26", "y24", "o22", "n2", "z07", "y05",
+    "o03", "z17", "y15", "n3", "o13", "z27", "y25", "o23", "n4", "y06", "o04", "y16", "n5", "o14", "A", "y26",
+    "o24", "y07", "o05", "y17", "o15", "y27", "o25", "o06", "o16", "o26", "o07", "o17", "o27", "c0", "p0", "h0",
     "c1", "p1", "h1", "c2", "p2", "h2", "Z0", "B", "Z1", "R0", "Z2", "C", "t00", "t01", "t02", "g0", "R1", "t10",
     "t11", "t12", "g1", "r0", "R2", "t20", "t21", "t22", "g2", "r1", "F0", "r2", "F1", "D", "F2",
 )

time: 113 us -> 114 us (level)
    pallas_call x1, Pallas kernels: 108 us -> 109 us  [local(): pl.pallas_call(block_kernel, out_shape=(jax.ShapeDtypeStruct((tiles, TILE...]
where the time goes in v5:
time: 114 us
  Pallas kernels  109 us (96%)
  local copies, waits for them, and re-layouts  4.15 us (4%)
    pallas_call x1, Pallas kernels, local(): pl.pallas_call(block_kernel, out_shape=(jax.ShapeDtypeStruct((tiles, TILE...  109 us
    unnamed x5, local copies, waits for them, and re-layouts  4.15 us

profile of v5, /device:TPU:1, one launch (start us, length us, event | category | flops | bytes accessed | tf_op | source)
XLA Modules:
  0.0 113.7 jit_solution(5285474344441322519)
XLA Ops:
  0.6 108.9 %block.1 = (bf16[3,96,384]{2,1,0:T(8,128)(2,1)}, bf16[3,3,96,384]{3,2,1,0:T(8,128)(2,1)}, f32[16]{0:T(128)}) custom-call(s32[3,12]{1,0:T(4,128)} %pattern_ref.1, f32[16]{0:T(128)} %hist_smem.1, bf16[288,384]{1,0:T(8,128)(2,1)} %x_hbm.1, bf16[3,48,384]{2,1,0:T(8,128)(2,1)} %w_hbm.1, f32[1,3072]{1,0:T(1,128)} %bitcast.9, f32[1,3072]{1,0:T(1,128)} %bitcast.10, ...), custom_call_target="tpu_custom_call" | custom-call | tf_op jit(solution)/shard_map/block/pallas_call | solution.py:653
  109.5 1.6 %copy.13 = bf16[288,384]{1,0:T(8,128)(2,1)} copy(bf16[288,384]{1,0:T(8,128)(2,1)} %bitcast.8) | data formatting | bytes 442368
  111.2 0.0 copy-start
  111.2 2.0 %copy.14 = bf16[3,288,384]{2,1,0:T(8,128)(2,1)} copy(bf16[3,288,384]{2,1,0:T(8,128)(2,1)} %bitcast.6) | data formatting | bytes 1327104
  113.2 0.0 copy-done
  113.2 0.5 copy.15
Async XLA Ops:
  111.2 2.0 %copy-start = (f32[16]{0:T(128)S(1)}, f32[16]{0:T(128)}, u32[]{:S(2)}) copy-start(f32[16]{0:T(128)} %get-tuple-element.14) | copy-start | bytes 196
